TPU v7x, 1024 devices: a whole 8x8x8 slice. The times are simulated.
1024 devices in a mesh: expert: 128 (over x, y, core), hidden: 8 (over z).
Axes of the slice: x: 8, y: 8, z: 8, core: 2. Of those that a mesh axis runs over, the one named last changes fastest.
Arguments:
- weight: bfloat16 [128, 1536, 4096], P('expert', 'hidden'), may hold values from -0.15625 to 0.15625
- scales: float32 [128, 12, 32], P('expert'), may hold values from 0.5 to 2
- act_own: bfloat16 [128, 128, 1536], P('expert', None, 'hidden'), may hold values from -6 to 6
- dy_own: bfloat16 [128, 128, 4096], P('expert'), may hold values from -6 to 6
- own_count: int32 [128], P('expert'), may hold values from 1 to 128, as said below
- act_help: bfloat16 [128, 32, 1536], P('expert', None, 'hidden'), may hold values from -6 to 6
- dy_help: bfloat16 [128, 32, 4096], P('expert'), may hold values from -24 to 24
- help_count: int32 [128], P('expert'), may hold values from 1 to 32, as said below
- hot: int32 [1], replicated, may hold values from 0 to 127
Outputs:
- y_own: bfloat16 [128, 128, 4096], P('expert', None, 'hidden')
- dact_own: bfloat16 [128, 128, 1536], P('expert', None, 'hidden')
- own_grad: bfloat16 [128, 1536, 4096], P('expert', 'hidden')
- y_help: bfloat16 [128, 32, 4096], P('expert', None, 'hidden')
- dact_help: bfloat16 [128, 32, 1536], P('expert', None, 'hidden')
- hot_grad: float32 [1536, 4096], P('hidden', 'expert')
Inputs may be any that keep to these rules, and one draw needn't show every extreme that they name: `own_count`: some expert has exactly 128 live rows. `help_count`: some group has exactly 32 live rows.
All inputs are finite; a program needn't handle non-finite values.
Results may differ from a plain program's by a relative error of at most 0.013.
Values may be sent and summed in bfloat16 or wider, within the bound.
A program may use at most 32 MiB of HBM per device.

v0:
```python
import jax
import jax.numpy as jnp
from jax import lax
from jax.sharding import Mesh
from jax.sharding import PartitionSpec as P

EXPERT = ("expert_0", "expert_1", "expert_2")


block_edge = 128


def from_root(block, axis, source):
    block = jnp.where(lax.axis_index(axis) == source, block, jnp.zeros_like(block))
    return lax.psum(block, axis)


def own_block(pieces, axes, sequence):
    dims = [lax.axis_size(a) for a in axes]
    pieces = pieces.reshape(*dims, *pieces.shape[1:])
    pieces = pieces.transpose(*sequence, *range(len(axes), pieces.ndim))
    pieces = pieces.reshape(-1, *pieces.shape[len(axes) :])
    for k in sequence:
        pieces = lax.psum_scatter(pieces, axes[k], scatter_dimension=0, tiled=True)
    return pieces[0]


def in_blocks(array, dim, size):
    before, after = (array.shape[:dim], array.shape[dim + 1 :])
    return jnp.moveaxis(array.reshape(*before, size, -1, *after), dim, 0)


def summed_rows(array, axes, sequence, dim):
    size = lax.axis_size(axes)
    return own_block(in_blocks(array, dim, size), axes, sequence)


def sent_and_summed(array, axis, dim):
    size = lax.axis_size(axis)
    pieces = lax.all_to_all(in_blocks(array, dim, size), axis, 0, 0, tiled=True)
    return jnp.sum(pieces.astype(jnp.float32), axis=0)


def sent_together(arrays, axis, dim, along):
    ends, at = ([], 0)
    for a in arrays[:-1]:
        at += a.shape[along]
        ends.append(at)
    both = jnp.concatenate(arrays, axis=along)
    return tuple(jnp.split(sent_and_summed(both, axis, dim), ends, axis=along))


def dequant(weight, scales, slice_start):
    height = weight.shape[1]
    depth = weight.shape[2]
    blocks = (slice_start + jnp.arange(height, dtype=jnp.int32)) // block_edge
    select = (blocks[:, None] == jnp.arange(scales.shape[1], dtype=jnp.int32)[None, :]).astype(
        jnp.float32
    )
    row_scale = jnp.einsum("fb,ebc->efc", select, scales, precision=lax.Precision.HIGHEST)
    shaped = weight.reshape(weight.shape[0], height, depth // block_edge, block_edge).astype(
        jnp.float32
    )
    shaped = shaped * row_scale[..., None]
    return shaped.reshape(weight.shape).astype(jnp.bfloat16)


def masked(values, count):
    live = jnp.arange(values.shape[1], dtype=jnp.int32)[None, :, None] < count[:, None, None]
    return jnp.where(live, values, jnp.zeros_like(values))


def body(weight, scales, act_own, dy_own, own_count, act_help, dy_help, help_count, hot):
    slice_start = lax.axis_index("hidden") * weight.shape[1]
    own_weight = dequant(weight, scales, slice_start)
    experts_here = weight.shape[0]
    hot_index = hot[0]
    hot_local = hot_index % experts_here
    hot_root = hot_index // experts_here
    own_rows = masked(act_own, own_count)
    own_grads = masked(dy_own, own_count)
    help_rows = masked(act_help, help_count)[0]
    help_grads = masked(dy_help, help_count)[0]
    partial_value = jnp.einsum(
        "erf,efd->erd", own_rows, own_weight, preferred_element_type=jnp.float32
    )
    dact = jnp.einsum("erd,efd->erf", own_grads, own_weight, preferred_element_type=jnp.float32)
    gradient = jnp.einsum("erf,erd->efd", own_rows, own_grads, preferred_element_type=jnp.float32)
    dact_own = dact.astype(jnp.bfloat16)
    own_grad = gradient.astype(jnp.bfloat16)
    chosen = lax.dynamic_index_in_dim(own_weight, hot_local, 0, keepdims=False)
    hot_weight = from_root(chosen, EXPERT, hot_root)
    help_partial_value = jnp.dot(help_rows, hot_weight, preferred_element_type=jnp.float32)
    dact = lax.dot_general(
        help_grads, hot_weight, (((1,), (1,)), ((), ())), preferred_element_type=jnp.float32
    )
    gradient = lax.dot_general(
        help_rows, help_grads, (((0,), (0,)), ((), ())), preferred_element_type=jnp.float32
    )
    summed = summed_rows(gradient, EXPERT, (2, 0, 1), 1)
    help_partial = help_partial_value[None]
    dact_help = dact.astype(jnp.bfloat16)[None]
    y_own, y_help = sent_together(
        (partial_value.astype(jnp.bfloat16), help_partial.astype(jnp.bfloat16)), "hidden", 2, 1
    )
    return (
        y_own.astype(jnp.bfloat16),
        dact_own,
        own_grad,
        y_help.astype(jnp.bfloat16),
        dact_help,
        summed,
    )


def solution(mesh):
    finer = Mesh(
        mesh.devices.reshape(8, 8, 2, mesh.shape["hidden"]),
        ("expert_0", "expert_1", "expert_2", "hidden"),
    )
    placed = (
        P(EXPERT, "hidden", None),
        P(EXPERT, None, None),
        P(EXPERT, None, "hidden"),
        P(EXPERT, None, None),
        P(EXPERT),
        P(EXPERT, None, "hidden"),
        P(EXPERT, None, None),
        P(EXPERT),
        P(),
    )
    return jax.shard_map(
        body,
        mesh=finer,
        in_specs=placed,
        out_specs=(
            P(EXPERT, None, "hidden"),
            P(EXPERT, None, "hidden"),
            P(EXPERT, "hidden", None),
            P(EXPERT, None, "hidden"),
            P(EXPERT, None, "hidden"),
            P("hidden", EXPERT),
        ),
        check_vma=False,
    )
```

profile of v0, /device:TPU:1, one launch (start us, length us, event | category | flops | bytes accessed | tf_op | source)
XLA Modules:
  0.0 316.7 jit_solution(10087944795170522439)
XLA Ops:
  8.0 0.0 reduce-scatter.4.cloned.1.call-start
  8.7 0.0 copy-start.4
  8.7 1.0 fusion.7
  9.8 0.8 dot_general.32
  10.6 0.5 copy.28
  11.1 0.0 copy-done.4
  11.1 0.7 convolution_bitcast_fusion
  11.8 3.5 %copy.29 = f32[128,192,32]{1,2,0:T(8,128)} copy(f32[128,192,32]{0,1,2:T(8,128)S(1)} %convolution_bitcast_fusion) | data formatting | bytes 6291456 | tf_op jit(solution)/shard_map/transpose | solution.py:30
  15.2 4.7 %copy.30 = f32[2,8,8,192,32]{3,4,2,1,0:T(8,128)} copy(f32[2,8,8,192,32]{3,4,0,2,1:T(8,128)} %bitcast.63) | data formatting | bytes 6291456 | tf_op jit(solution)/shard_map/transpose | solution.py:21
  20.0 0.0 copy-start.5
  20.0 0.0 reduce-scatter.4.cloned.1.call-update
  20.0 0.0 all-reduce.2.cloned.1.call-start
  20.7 0.0 copy-done.5
  20.7 0.2 fusion.8
  21.0 0.9 mul.24
  21.8 2.4 mul.25
  24.2 4.1 %broadcast_select_fusion = (bf16[192,4096]{1,0:T(8,128)(2,1)}, bf16[192,4096]{1,0:T(8,128)(2,1)S(1)}) fusion(pred[]{:T(512)S(6)} %eq.21, f32[1,192,4096]{2,1,0:T(8,128)} %mul.25, bf16[1,192,4096]{2,1,0:T(8,128)(2,1)} %param.9), kind=kLoop, calls=%fused_computation.7 | loop fusion | flops 3145728 | bytes 7864321 | tf_op jit(solution)/shard_map/jit(_where)/select_n | solution.py:14
  28.4 0.0 copy-start.3
  28.4 0.0 all-reduce.2.cloned.1.call-update
  28.4 0.0 reduce-scatter.6.cloned.1.call-start
  28.4 29.1 %reduce-scatter.4.cloned.1.call-done = f32[64,192,32]{1,2,0:T(8,128)} async-done(((f32[128,192,32]{1,2,0:T(8,128)}), f32[64,192,32]{1,2,0:T(8,128)}) %reduce-scatter.4.cloned.1.call-update) | async-done | bytes 1572880 | tf_op jit(solution)/shard_map/reduce_scatter | solution.py:24
  57.5 0.0 reduce-scatter.6.cloned.1.call-update
  58.2 0.0 copy-done.3
  58.2 0.5 convolution_convert_fusion.1
  58.7 0.4 copy.33
  59.1 0.3 copy.26
  59.4 198.2 %all-reduce.2.cloned.1.call-done = bf16[192,4096]{1,0:T(8,128)(2,1)} async-done(((bf16[192,4096]{1,0:T(8,128)(2,1)}), bf16[192,4096]{1,0:T(8,128)(2,1)}) %all-reduce.2.cloned.1.call-update) | async-done | bytes 1572880 | tf_op jit(solution)/shard_map/psum | solution.py:15
  257.6 1.8 convolution_convert_fusion.2
  259.4 0.1 copy.34
  259.5 0.1 copy.27
  259.6 1.2 maximum_bitcast_fusion
  260.8 7.5 %all-to-all-start = ((bf16[8,1,160,512]{3,2,1,0:T(8,128)(2,1)}), bf16[8,1,160,512]{3,2,1,0:T(8,128)(2,1)S(1)}, u32[]{:S(2)}, u32[]{:S(2)}) async-start(bf16[8,1,160,512]{3,2,1,0:T(8,128)(2,1)} %maximum_bitcast_fusion), calls=%async_computation | async-start | bytes 2621440 | tf_op jit(solution)/shard_map/all_to_all | solution.py:40
  268.4 0.0 reduce-scatter.8.cloned.1.call-start
  268.4 0.0 reduce-scatter.6.cloned.1.call-done
  268.4 0.7 reduce-scatter.8.cloned.1.call-update
  269.1 0.0 copy-start.1
  269.1 2.6 fusion.2
  271.7 0.0 copy-done.1
  271.7 0.0 copy-start.2
  271.7 1.8 fusion
  273.5 0.0 copy-done
  273.5 0.0 copy-done.2
  273.5 1.2 fusion.3
  274.7 28.4 %all-to-all-done = bf16[8,1,160,512]{3,2,1,0:T(8,128)(2,1)S(1)} async-done(((bf16[8,1,160,512]{3,2,1,0:T(8,128)(2,1)}), bf16[8,1,160,512]{3,2,1,0:T(8,128)(2,1)S(1)}, u32[]{:S(2)}, u32[]{:S(2)}) %all-to-all-start) | async-done | bytes 1310752 | tf_op jit(solution)/shard_map/all_to_all | solution.py:40
  303.2 0.2 reduce.1
  303.4 0.7 split.10
  304.0 0.6 split.11
  304.6 4.9 %reduce-scatter.8.cloned.1.call-done = f32[1,192,32]{1,2,0:T(8,128)} async-done(((f32[8,192,32]{1,2,0:T(8,128)}), f32[1,192,32]{1,2,0:T(8,128)}) %reduce-scatter.8.cloned.1.call-update) | async-done | bytes 24592 | tf_op jit(solution)/shard_map/reduce_scatter | solution.py:24
  (4 shorter events, 0.0 us)
Async XLA Ops:
  8.0 49.5 %reduce-scatter.4.cloned.1.call-start = ((), (), s32[]{:S(2)}) async-start(), calls=%async_computation.5 | async-start | bytes 6291456 | tf_op jit(solution)/shard_map/reduce_scatter | solution.py:24
  8.7 2.4 copy-start.4
  20.0 0.8 copy-start.5
  20.0 237.6 %all-reduce.2.cloned.1.call-start = ((), (), s32[]{:S(2)}) async-start(), calls=%async_computation.4 | async-start | bytes 3145728 | tf_op jit(solution)/shard_map/psum | solution.py:15
  28.4 29.8 %copy-start.3 = (bf16[1,128,192]{1,2,0:T(8,128)(2,1)S(1)}, bf16[1,128,192]{1,2,0:T(8,128)(2,1)}, u32[]{:S(2)}) copy-start(bf16[1,128,192]{1,2,0:T(8,128)(2,1)} %param.11) | copy-start | bytes 147460
  28.4 240.0 %reduce-scatter.6.cloned.1.call-start = ((), (), s32[]{:S(2)}) async-start(), calls=%async_computation.6 | async-start | bytes 2359296 | tf_op jit(solution)/shard_map/reduce_scatter | solution.py:24
  260.8 42.3 %all-to-all-start = ((bf16[8,1,160,512]{3,2,1,0:T(8,128)(2,1)}), bf16[8,1,160,512]{3,2,1,0:T(8,128)(2,1)S(1)}, u32[]{:S(2)}, u32[]{:S(2)}) async-start(bf16[8,1,160,512]{3,2,1,0:T(8,128)(2,1)} %maximum_bitcast_fusion), calls=%async_computation | async-start | bytes 2621440 | tf_op jit(solution)/shard_map/all_to_all | solution.py:40
  268.4 41.2 %reduce-scatter.8.cloned.1.call-start = ((), (), s32[]{:S(2)}) async-start(), calls=%async_computation.7 | async-start | bytes 294912 | tf_op jit(solution)/shard_map/reduce_scatter | solution.py:24
  269.1 2.6 copy-start.1
  271.7 1.8 copy-start
  271.7 1.8 copy-start.2
Sparse Core Ops, SparseCore 0:
  20.1 37.3 reduce-scatter.3
  60.9 43.4 reduce-scatter.5
  273.1 36.3 reduce-scatter.7
Sparse Core Ops, SparseCore 1:
  28.5 229.0 all-reduce.1
where the time goes:
time: 321 us; the launch traced here: 317 us
  waiting for transfers between devices  261 us (81%)
  between operations  17.3 us (5%)
  local copies, waits for them, and re-layouts  15 us (5%)
  matrix products  8.83 us (3%)
  starting transfers between devices  7.69 us (2%)
  other arithmetic  6.62 us (2%)
    psum x1, waiting for transfers between devices, from_root(): return lax.psum(block, axis)  198 us
    reduce_scatter x3, waiting for transfers between devices, own_block(): pieces = lax.psum_scatter(pieces, axes[k], scatter_dimension=0, tiled=True)  34 us
    all_to_all x1, waiting for transfers between devices, sent_and_summed(): pieces = lax.all_to_all(in_blocks(array, dim, size), axis, 0, 0, tiled=True)  28.4 us
    all_to_all x1, starting transfers between devices, sent_and_summed(): pieces = lax.all_to_all(in_blocks(array, dim, size), axis, 0, 0, tiled=True)  7.53 us
  transfers between devices with their start and end apart: 5, of which 4 were waited for; matrix products, arithmetic and copies ran while one was open for 6% of the time, Pallas kernels for 0%

commit v1 on v0

v1 whole, which is shorter than its diff:
```python
import functools

import jax
import jax.numpy as jnp
from jax import lax
from jax.experimental import pallas as pl
from jax.experimental.pallas import tpu as pltpu
from jax.sharding import PartitionSpec as P

MESH = pl.DeviceIdType.MESH
BF16 = jnp.bfloat16
F32 = jnp.float32
LANES = 128
NT = (((1,), (1,)), ((), ()))
TN = (((0,), (0,)), ((), ()))


def kernel(
    cfg,
    hot, own_count, help_count, scales, act_own, act_help, weight, dy_own, dy_help,
    y_own, dact_own, own_grad, y_help, dact_help, hot_grad,
    w_v, dyo_v, deq, own_a, pairs_a, pairs_g, mine, give, got, r1, s2, r2, wf,
    yp, ry, og, gd, ad, dw, rd, ys, ryh, da_give, da_got,
    load_sem, ex_s, ex_r, pair_s, pair_r, xa_s, xa_r, xg_s, xg_r, z_s, z_r,
    s1_s, s1_r, s2_s, s2_r, s3_s, s3_r, s4_s, s4_r, dw_s, dw_r, yh_s, yh_r, da_s, da_r,
):
    n, nz, ff, rows, hrows, depth = cfg
    half = depth // 2
    zblock = depth // nz
    xblock = depth // n
    cols = xblock // (2 * n)
    chunk = 2 * ff // n
    per = ff // chunk
    e, z = lax.axis_index("expert"), lax.axis_index("hidden")
    x, y, c = lax.div(e, 2 * n), lax.rem(lax.div(e, 2), n), lax.rem(e, 2)
    o = 1 - c

    def at(px, py, pc, pz):
        return ((px * n + py) * 2 + pc, pz)

    first = o * x + c * y
    second = o * y + c * x
    first_p = o * y + c * x

    def along_first(p):
        return at(o * p + c * x, o * y + c * p, c, z)

    def along_second(p):
        return at(o * x + c * p, o * p + c * y, c, z)

    def along_x(p):
        return at(p, y, c, z)

    partner = at(x, y, o, z)

    def loop(low, high, body):
        def step(i, carry):
            body(i)
            return carry

        lax.fori_loop(low, high, step, 0)

    def nth(i, count):
        turn = jnp.where(lax.rem(i, 2) == 0, lax.div(i, 2) + 1, count - lax.div(i + 1, 2))
        return jnp.where(i == count - 1, 0, turn)

    def remote(src, dst, send, recv, device):
        return pltpu.make_async_remote_copy(
            src_ref=src, dst_ref=dst, send_sem=send, recv_sem=recv,
            device_id=device, device_id_type=MESH,
        )

    col_p = pl.multiple_of(o * half, half)
    col_m = pl.multiple_of(c * half, half)
    load_wp = pltpu.make_async_copy(
        weight.at[:, pl.ds(col_p, half)], w_v.at[:, pl.ds(col_p, half)], load_sem.at[0]
    )
    load_wm = pltpu.make_async_copy(
        weight.at[:, pl.ds(col_m, half)], w_v.at[:, pl.ds(col_m, half)], load_sem.at[1]
    )
    load_g = pltpu.make_async_copy(
        dy_help.at[:, pl.ds(col_m, half)], pairs_g.at[pl.ds(0, hrows)], load_sem.at[2]
    )
    load_gd = pltpu.make_async_copy(
        dy_help.at[:, pl.ds(pl.multiple_of(x * xblock, xblock), xblock)], gd.at[x], load_sem.at[3]
    )
    load_dyo = pltpu.make_async_copy(dy_own, dyo_v, load_sem.at[4])
    for load in (load_wp, load_wm, load_gd, load_g, load_dyo):
        load.start()

    barrier = pltpu.get_barrier_semaphore()

    def greet(device):
        pl.semaphore_signal(barrier, inc=1, device_id=device, device_id_type=MESH)

    def greet_plane(d):
        px, py = lax.rem(x + d, n), lax.rem(y + d, n)
        greet(at(px, y, c, z))
        greet(at(x, py, c, z))
        greet(at(x, py, o, z))

    def greet_line(d):
        pz = lax.rem(z + d, nz)
        greet(at(x, y, c, pz))
        greet(at(x, y, o, pz))

    greet(partner)
    loop(1, n, greet_plane)
    loop(1, nz, greet_line)

    live_help = lax.broadcasted_iota(jnp.int32, (hrows, ff), 0) < help_count[0]
    live_own = lax.broadcasted_iota(jnp.int32, (rows, ff), 0) < own_count[0]
    help_a = jnp.where(live_help, act_help[...].astype(F32), 0.0).astype(BF16)
    own_a[...] = jnp.where(live_own, act_own[...].astype(F32), 0.0).astype(BF16)
    pairs_a[pl.ds(0, hrows), :] = help_a
    ad[x] = help_a

    flag = jnp.where(hot[0] == e, 1.0, 0.0).astype(F32)

    def scaled(col_base, at_first, dest, i):
        t = lax.rem(at_first + nth(i, n), n)
        for k in range(2):
            tile = lax.div(col_base, LANES) + 2 * t + k
            col = pl.multiple_of(tile * LANES, LANES)
            for part in range(3):
                third = ff // 3
                span = pl.ds(part * third, third)
                scale = scales[lax.div(3 * z + part, 2), tile]
                wide = w_v[span, pl.ds(col, LANES)].astype(F32) * scale
                deq[span, pl.ds(col, LANES)] = wide.astype(BF16)
                dest[2 * i + k, span, :] = (wide * flag).astype(BF16)

    groups = min(4, n)
    each = n // groups

    pl.semaphore_wait(barrier, 3 * (n - 1) + 2 * (nz - 1) + 1)

    def send_x(d):
        p = lax.rem(x + d, n)
        block = pl.ds(pl.multiple_of(p * xblock, xblock), xblock)
        remote(dy_help.at[:, block], gd.at[x], xg_s.at[p], xg_r.at[x], along_x(p)).start()
        remote(
            pairs_a.at[pl.ds(0, hrows)], ad.at[x], xa_s.at[p], xa_r.at[x], along_x(p)
        ).start()

    pair_g = remote(
        dy_help.at[:, pl.ds(col_p, half)], pairs_g.at[pl.ds(hrows, hrows)],
        pair_s.at[0], pair_r.at[0], partner,
    )
    pair_a = remote(
        pairs_a.at[pl.ds(0, hrows)], pairs_a.at[pl.ds(hrows, hrows)],
        pair_s.at[1], pair_r.at[1], partner,
    )
    pair_a.start()

    load_wp.wait()

    def exchange(q):
        tiles = pl.ds(q * 2 * each, 2 * each)
        return remote(give.at[tiles], got.at[tiles], ex_s.at[q], ex_r.at[q], partner)

    def give_group(q):
        for j in range(each):
            scaled(col_p, first_p, give, q * each + j)
        exchange(q).start()

    loop(0, groups, give_group)
    loop(1, n, send_x)
    pair_g.start()
    load_wm.wait()
    loop(0, n, functools.partial(scaled, col_m, first, mine))

    def send_first(i):
        t = lax.rem(first + nth(i, n), n)
        tiles = pl.ds(2 * i, 2)
        mine[tiles] = mine[tiles] + got[tiles]
        remote(mine.at[tiles], r1.at[first], s1_s.at[t], s1_r.at[first], along_first(t)).start()

    def own_partial(pz):
        block = pl.ds(pl.multiple_of(pz * zblock, zblock), zblock)
        return jnp.dot(own_a[...], deq[:, block], preferred_element_type=F32).astype(BF16)

    def send_z(i):
        pz = lax.rem(z + nth(i, nz), nz)
        yp[pz] = own_partial(pz)
        remote(yp.at[pz], ry.at[z], z_s.at[pz], z_r.at[z], at(x, y, c, pz)).start()

    loop(0, nz - 1, send_z)
    ry[z] = own_partial(z)

    for q in range(groups):
        exchange(q).wait_recv()
        for j in range(each):
            i = q * each + j
            if i < n - 1:
                send_first(i)
            else:
                tiles = pl.ds(2 * i, 2)
                r1[first] = mine[tiles] + got[tiles]

    load_dyo.wait()
    kblock = 512

    def dact_step(j, total):
        block = pl.ds(pl.multiple_of(j * kblock, kblock), kblock)
        return total + lax.dot_general(
            dyo_v[:, block], deq[:, block], NT, preferred_element_type=F32
        )

    total = lax.fori_loop(0, depth // kblock, dact_step, jnp.zeros((rows, ff), F32))
    dact_own[...] = jnp.where(live_own, total, 0.0).astype(BF16)

    def grad_step(j):
        block = pl.ds(pl.multiple_of(j * kblock, kblock), kblock)
        og[:, block] = lax.dot_general(
            own_a[...], dyo_v[:, block], TN, preferred_element_type=F32
        ).astype(BF16)

    loop(0, depth // kblock, grad_step)
    store_og = pltpu.make_async_copy(og, own_grad, load_sem.at[5])
    store_og.start()

    load_gd.wait()

    def wait_x(d):
        p = lax.rem(x + d, n)
        remote(gd.at[p], gd.at[p], xg_s.at[p], xg_r.at[p], along_x(p)).wait_recv()
        remote(ad.at[p], ad.at[p], xa_s.at[p], xa_r.at[p], along_x(p)).wait_recv()

    loop(1, n, wait_x)
    dw[...] = lax.dot_general(
        gd[...].reshape(n * hrows, xblock), ad[...].reshape(n * hrows, ff), TN,
        preferred_element_type=F32,
    )

    def wait_first(d):
        p = lax.rem(first + d, n)
        remote(r1.at[p], r1.at[p], s1_s.at[p], s1_r.at[p], along_first(p)).wait_recv()

    loop(1, n, wait_first)

    def sum_first(i):
        k, span = lax.rem(i, 2), pl.ds(pl.multiple_of(lax.div(i, 2) * chunk, chunk), chunk)
        piece = r1[0, k, span, :].astype(F32)
        for p in range(1, n):
            piece = piece + r1[p, k, span, :].astype(F32)
        s2[k, span, :] = piece.astype(BF16)

    loop(0, 2 * per, sum_first)

    def place(p):
        return lax.div(p, per), pl.ds(pl.multiple_of(lax.rem(p, per) * chunk, chunk), chunk)

    def send_second(i):
        p = lax.rem(second + nth(i, n), n)
        k, span = place(p)
        remote(
            s2.at[k, span], r2.at[second], s2_s.at[p], s2_r.at[second], along_second(p)
        ).start()

    loop(0, n - 1, send_second)
    my_k, my_span = place(second)
    r2[second] = s2[my_k, my_span, :]

    def wait_second(d):
        p = lax.rem(second + d, n)
        remote(r2.at[p], r2.at[p], s2_s.at[p], s2_r.at[p], along_second(p)).wait_recv()

    loop(1, n, wait_second)
    piece = r2[0].astype(F32)
    for p in range(1, n):
        piece = piece + r2[p].astype(F32)
    spot = wf.at[2 * first + my_k, my_span]
    spot[...] = piece.astype(BF16)

    def send_third(i):
        p = lax.rem(second + nth(i, n), n)
        remote(spot, spot, s3_s.at[p], s3_r.at[second], along_second(p)).start()

    loop(0, n - 1, send_third)

    def send_dw(i):
        p = lax.rem(y + nth(i, n), n)
        for pc in range(2):
            part = pl.ds(pl.multiple_of((2 * p + pc) * cols, cols), cols)
            remote(
                dw.at[part], rd.at[2 * y + c], dw_s.at[2 * p + pc], dw_r.at[2 * y + c],
                at(x, p, pc, z),
            ).start()

    loop(0, n - 1, send_dw)
    mine_part = pl.ds(pl.multiple_of((2 * y + c) * cols, cols), cols)
    other_part = pl.ds(pl.multiple_of((2 * y + o) * cols, cols), cols)
    dw_pair = remote(
        dw.at[other_part], rd.at[2 * y + c], dw_s.at[2 * y + o], dw_r.at[2 * y + c], partner
    )
    dw_pair.start()
    rd[2 * y + c] = dw[mine_part, :]

    def wait_third(d):
        p = lax.rem(second + d, n)
        k, span = place(p)
        there = wf.at[2 * first + k, span]
        remote(there, there, s3_s.at[p], s3_r.at[p], along_second(p)).wait_recv()

    loop(1, n, wait_third)

    whole = wf.at[pl.ds(2 * first, 2)]

    def send_fourth(i):
        p = lax.rem(first + nth(i, n), n)
        remote(whole, whole, s4_s.at[p], s4_r.at[first], along_first(p)).start()

    loop(0, n - 1, send_fourth)

    def wait_z(d):
        p = lax.rem(z + d, nz)
        remote(ry.at[p], ry.at[p], z_s.at[p], z_r.at[p], at(x, y, c, p)).wait_recv()

    loop(1, nz, wait_z)

    def sum_z(i):
        span = pl.ds(pl.multiple_of(i * 16, 16), 16)
        piece = ry[0, span, :].astype(F32)
        for p in range(1, nz):
            piece = piece + ry[p, span, :].astype(F32)
        y_own[span, :] = piece.astype(BF16)

    loop(0, rows // 16, sum_z)

    def wait_dw(d):
        p = lax.rem(y + d, n)
        for pc in range(2):
            slot = 2 * p + pc
            remote(
                rd.at[slot], rd.at[slot], dw_s.at[slot], dw_r.at[slot], at(x, p, pc, z)
            ).wait_recv()

    loop(1, n, wait_dw)
    remote(
        rd.at[2 * y + o], rd.at[2 * y + o], dw_s.at[2 * y + o], dw_r.at[2 * y + o], partner
    ).wait_recv()
    total = rd[0]
    for p in range(1, 2 * n):
        total = total + rd[p]
    hot_grad[...] = total.T

    load_g.wait()
    pair_g.wait_recv()
    pair_a.wait_recv()
    blocks = half // zblock
    tiles_per = zblock // LANES

    def wait_fourth(p):
        there = wf.at[pl.ds(2 * p, 2)]
        remote(there, there, s4_s.at[p], s4_r.at[p], along_first(p)).wait_recv()

    da = jnp.zeros((2 * hrows, ff), F32)
    for m in range(blocks):
        pz = c * blocks + m
        for p in range(m * tiles_per // 2, (m + 1) * tiles_per // 2):
            pl.when(first != p)(functools.partial(wait_fourth, p))
        block = jnp.concatenate([wf[m * tiles_per + j] for j in range(tiles_per)], axis=1)
        out = jnp.dot(pairs_a[...], block, preferred_element_type=F32).astype(BF16)
        ys[m] = out.reshape(2, hrows, zblock)
        remote(
            ys.at[m, 1], ryh.at[z], yh_s.at[2 * m + 1], yh_r.at[z], at(x, y, o, pz)
        ).start()

        @pl.when(pz != z)
        def _():
            remote(
                ys.at[m, 0], ryh.at[z], yh_s.at[2 * m], yh_r.at[z], at(x, y, c, pz)
            ).start()

        @pl.when(pz == z)
        def _():
            ryh[z] = ys[m, 0]

        da = da + lax.dot_general(
            pairs_g[:, m * zblock : (m + 1) * zblock], block, NT, preferred_element_type=F32
        )
    da_give[...] = da[hrows:]
    da_copy = remote(da_give, da_got, da_s.at[0], da_r.at[0], partner)
    da_copy.start()

    source = lax.div(z, blocks)

    def wait_yh(p):
        @pl.when((p != z) | (source != c))
        def _():
            remote(
                ryh.at[p], ryh.at[p], yh_s.at[0], yh_r.at[p], at(x, y, source, p)
            ).wait_recv()

    da_copy.wait_recv()
    dact_help[...] = jnp.where(live_help, da[:hrows] + da_got[...], 0.0).astype(BF16)

    loop(0, nz, wait_yh)
    piece = ryh[0].astype(F32)
    for p in range(1, nz):
        piece = piece + ryh[p].astype(F32)
    y_help[...] = piece.astype(BF16)

    store_og.wait()
    pair_a.wait_send()
    pair_g.wait_send()
    dw_pair.wait_send()
    da_copy.wait_send()

    def drain_exchange(q):
        exchange(q).wait_send()

    loop(0, groups, drain_exchange)

    def drain_plane(d):
        px, pf, ps, py = (lax.rem(v + d, n) for v in (x, first, second, y))
        remote(gd.at[px], gd.at[px], xg_s.at[px], xg_r.at[px], along_x(px)).wait_send()
        remote(ad.at[px], ad.at[px], xa_s.at[px], xa_r.at[px], along_x(px)).wait_send()
        remote(r1.at[pf], r1.at[pf], s1_s.at[pf], s1_r.at[pf], along_first(pf)).wait_send()
        remote(r2.at[ps], r2.at[ps], s2_s.at[ps], s2_r.at[ps], along_second(ps)).wait_send()
        remote(spot, spot, s3_s.at[ps], s3_r.at[ps], along_second(ps)).wait_send()
        remote(whole, whole, s4_s.at[pf], s4_r.at[pf], along_first(pf)).wait_send()
        for pc in range(2):
            slot = 2 * py + pc
            remote(
                rd.at[slot], rd.at[slot], dw_s.at[slot], dw_r.at[slot], at(x, py, pc, z)
            ).wait_send()

    loop(1, n, drain_plane)

    def drain_line(d):
        p = lax.rem(z + d, nz)
        remote(ry.at[p], ry.at[p], z_s.at[p], z_r.at[p], at(x, y, c, p)).wait_send()

    loop(1, nz, drain_line)
    for m in range(blocks):
        pz = c * blocks + m
        remote(
            ys.at[m, 1], ryh.at[z], yh_s.at[2 * m + 1], yh_r.at[z], at(x, y, o, pz)
        ).wait_send()

        @pl.when(pz != z)
        def _():
            remote(
                ys.at[m, 0], ryh.at[z], yh_s.at[2 * m], yh_r.at[z], at(x, y, c, pz)
            ).wait_send()


def solution(mesh):
    nz = mesh.shape["hidden"]
    n = 1
    while 2 * n * n < mesh.shape["expert"]:
        n += 1

    def body(weight, scales, act_own, dy_own, own_count, act_help, dy_help, help_count, hot):
        ff, depth = weight.shape[1:]
        rows, hrows = act_own.shape[1], act_help.shape[1]
        half, zblock, xblock = depth // 2, depth // nz, depth // n
        cols, chunk = xblock // (2 * n), 2 * ff // n
        tiles = half // LANES
        groups = min(4, n)
        blocks = half // zblock
        vmem = pltpu.VMEM
        dma = pltpu.SemaphoreType.DMA
        smem = pl.BlockSpec(memory_space=pltpu.SMEM)
        near = pl.BlockSpec(memory_space=pltpu.VMEM)
        far = pl.BlockSpec(memory_space=pl.ANY)
        outs = pl.pallas_call(
            functools.partial(kernel, (n, nz, ff, rows, hrows, depth)),
            out_shape=(
                jax.ShapeDtypeStruct((rows, zblock), BF16),
                jax.ShapeDtypeStruct((rows, ff), BF16),
                jax.ShapeDtypeStruct((ff, depth), BF16),
                jax.ShapeDtypeStruct((hrows, zblock), BF16),
                jax.ShapeDtypeStruct((hrows, ff), BF16),
                jax.ShapeDtypeStruct((ff, cols), F32),
            ),
            in_specs=[smem] * 4 + [near] * 2 + [far] * 3,
            out_specs=(near, near, far, near, near, near),
            scratch_shapes=[
                vmem((ff, depth), BF16),
                vmem((rows, depth), BF16),
                vmem((ff, depth), BF16),
                vmem((rows, ff), BF16),
                vmem((2 * hrows, ff), BF16),
                vmem((2 * hrows, half), BF16),
                vmem((tiles, ff, LANES), BF16),
                vmem((tiles, ff, LANES), BF16),
                vmem((tiles, ff, LANES), BF16),
                vmem((n, 2, ff, LANES), BF16),
                vmem((2, ff, LANES), BF16),
                vmem((n, chunk, LANES), BF16),
                vmem((tiles, ff, LANES), BF16),
                vmem((nz, rows, zblock), BF16),
                vmem((nz, rows, zblock), BF16),
                vmem((ff, depth), BF16),
                vmem((n, hrows, xblock), BF16),
                vmem((n, hrows, ff), BF16),
                vmem((xblock, ff), F32),
                vmem((2 * n, cols, ff), F32),
                vmem((blocks, 2, hrows, zblock), BF16),
                vmem((nz, hrows, zblock), BF16),
                vmem((hrows, ff), F32),
                vmem((hrows, ff), F32),
                dma((6,)),
                dma((groups,)), dma((groups,)),
                dma((2,)), dma((2,)),
                dma((n,)), dma((n,)),
                dma((n,)), dma((n,)),
                dma((nz,)), dma((nz,)),
                dma((n,)), dma((n,)),
                dma((n,)), dma((n,)),
                dma((n,)), dma((n,)),
                dma((n,)), dma((n,)),
                dma((2 * n,)), dma((2 * n,)),
                dma((2 * blocks,)), dma((nz,)),
                dma((1,)), dma((1,)),
            ],
            compiler_params=pltpu.CompilerParams(collective_id=0, has_side_effects=True),
            name="moe_step",
        )(
            hot, own_count, help_count, scales[0], act_own[0], act_help[0],
            weight[0], dy_own[0], dy_help[0],
        )
        own, dact_own, own_grad, helped, dact_help, hot_grad = outs
        return own[None], dact_own[None], own_grad[None], helped[None], dact_help[None], hot_grad

    return jax.shard_map(
        body,
        mesh=mesh,
        in_specs=(
            P("expert", "hidden", None),
            P("expert", None, None),
            P("expert", None, "hidden"),
            P("expert", None, None),
            P("expert"),
            P("expert", None, "hidden"),
            P("expert", None, None),
            P("expert"),
            P(),
        ),
        out_specs=(
            P("expert", None, "hidden"),
            P("expert", None, "hidden"),
            P("expert", "hidden", None),
            P("expert", None, "hidden"),
            P("expert", None, "hidden"),
            P("hidden", "expert"),
        ),
        check_vma=False,
    )
```

time: 321 us -> 94.7 us (0.30)
  the two profiles are of different devices: /device:TPU:1 before, /device:TPU:10 now
where the time goes in v1:
time: 94.7 us; the launch traced here: 94.3 us
  Pallas kernels  80.2 us (85%)
  local copies, waits for them, and re-layouts  11.5 us (12%)
  between operations  2.58 us (3%)
    pallas_call x1, Pallas kernels, body(): pl.pallas_call(functools.partial(kernel, (n, nz, ff, rows, hrows, depth))...  80.2 us
    unnamed x12, local copies, waits for them, and re-layouts  11.5 us

profile of v1, /device:TPU:10, one launch (start us, length us, event | category | flops | bytes accessed | tf_op | source)
XLA Modules:
  0.0 94.3 jit_solution(7646266650205019319)
XLA Ops:
  2.6 1.3 %copy.20 = f32[1,12,32]{2,1,0:T(8,128)} copy(f32[1,12,32]{2,0,1:T(1,128)} %param.10) | data formatting | bytes 3072
  3.9 1.5 %copy.15 = bf16[1,128,192]{2,1,0:T(8,128)(2,1)} copy(bf16[1,128,192]{1,2,0:T(8,128)(2,1)} %param.11) | data formatting | bytes 98304 | tf_op args[2]
  5.4 80.2 %moe_step.1 = (bf16[128,512]{1,0:T(8,128)(2,1)}, bf16[128,192]{1,0:T(8,128)(2,1)}, bf16[192,4096]{1,0:T(8,128)(2,1)}, bf16[32,512]{1,0:T(8,128)(2,1)}, bf16[32,192]{1,0:T(8,128)(2,1)}, /*index=5*/f32[192,32]{1,0:T(8,128)}) custom-call(s32[1]{0:T(128)S(6)} %copy.27.hot, s32[1]{0:T(128)S(6)} %copy.25.own_count, s32[1]{0:T(128)S(6)} %copy.26.help_count, ...), custom_call_target="tpu_custom_call" | custom-call | tf_op jit(solution)/shard_map/moe_step/pallas_call | solution.py:469
  85.6 1.6 %copy.16 = bf16[1,128,192]{1,2,0:T(8,128)(2,1)} copy(bf16[1,128,192]{2,1,0:T(8,128)(2,1)} %bitcast.19) | data formatting | bytes 98304
  87.2 1.6 %copy.17 = f32[192,32]{0,1:T(8,128)} copy(f32[192,32]{1,0:T(8,128)} %get-tuple-element.23) | data formatting | bytes 49152
  88.8 1.6 %copy.28 = bf16[1,128,512]{2,1,0:T(8,128)(2,1)} copy(bf16[1,128,512]{2,1,0:T(8,128)(2,1)} %bitcast.18) | data formatting | bytes 262144
  90.3 0.0 copy-start
  90.3 0.0 copy-start.1
  90.3 2.7 %copy.29 = bf16[1,192,4096]{2,1,0:T(8,128)(2,1)} copy(bf16[1,192,4096]{2,1,0:T(8,128)(2,1)} %bitcast.14) | data formatting | bytes 3145728
  93.0 0.0 copy-done
  93.0 0.6 copy.30
  93.7 0.0 copy-done.1
  93.7 0.6 copy.31
Async XLA Ops:
  90.3 2.7 %copy-start = (bf16[32,512]{1,0:T(8,128)(2,1)S(1)}, bf16[32,512]{1,0:T(8,128)(2,1)}, u32[]{:S(2)}) copy-start(bf16[32,512]{1,0:T(8,128)(2,1)} %get-tuple-element.15) | copy-start | bytes 98308
  90.3 3.3 %copy-start.1 = (bf16[32,192]{1,0:T(8,128)(2,1)S(1)}, bf16[32,192]{1,0:T(8,128)(2,1)}, u32[]{:S(2)}) copy-start(bf16[32,192]{1,0:T(8,128)(2,1)} %get-tuple-element.16) | copy-start | bytes 36868

commit v2 on v1

v2 whole, which is shorter than its diff:
```python
import functools

import jax
import jax.numpy as jnp
from jax import lax
from jax.experimental import pallas as pl
from jax.experimental.pallas import tpu as pltpu
from jax.sharding import PartitionSpec as P

MESH = pl.DeviceIdType.MESH
BF16 = jnp.bfloat16
F32 = jnp.float32
LANES = 128
NT = (((1,), (1,)), ((), ()))
TN = (((0,), (0,)), ((), ()))


def kernel(
    cfg,
    hot_h, own_count_h, help_count_h, scales_h, act_own_h, act_help_h, weight, dy_own, dy_help,
    y_own, dact_own, y_help, dact_help, hot_grad,
    hot, own_count, help_count, scales, ao_v, ah_v,
    w_v, dyo_v, deq, own_a, pairs_a, pairs_g, mine, give, got, r1, s2, r2, wf,
    yp, ry, gd, ad, dw, rd, ys, ryh, da_give, da_got,
    load_sem, ex_s, ex_r, pair_s, pair_r, xa_s, xa_r, xg_s, xg_r, fa_s, fa_r, z_s, z_r,
    s1_s, s1_r, s2_s, s2_r, s3_s, s3_r, s4_s, s4_r, dw_s, dw_r, yh_s, yh_r, da_s, da_r,
):
    n, nz, ff, rows, hrows, depth = cfg
    half = depth // 2
    zblock = depth // nz
    xblock = depth // n
    xhalf = xblock // 2
    cols = xblock // (2 * n)
    chunk = 2 * ff // n
    per = ff // chunk
    both = 2 if per > 1 else 1
    parts = n // both
    tall = both * chunk
    e, z = lax.axis_index("expert"), lax.axis_index("hidden")
    x, y, c = lax.div(e, 2 * n), lax.rem(lax.div(e, 2), n), lax.rem(e, 2)
    o = 1 - c

    def at(px, py, pc, pz):
        return ((px * n + py) * 2 + pc, pz)

    first = o * x + c * y
    second = o * y + c * x
    first_p = o * y + c * x

    def along_first(p):
        return at(o * p + c * x, o * y + c * p, c, z)

    def along_second(p):
        return at(o * x + c * p, o * p + c * y, c, z)

    def along_x(p):
        return at(p, y, c, z)

    partner = at(x, y, o, z)

    def loop(low, high, body):
        def step(i, carry):
            body(i)
            return carry

        lax.fori_loop(low, high, step, 0)

    def nth(i, count):
        turn = jnp.where(lax.rem(i, 2) == 0, lax.div(i, 2) + 1, count - lax.div(i + 1, 2))
        return jnp.where(i == count - 1, 0, turn)

    def remote(src, dst, send, recv, device):
        return pltpu.make_async_remote_copy(
            src_ref=src, dst_ref=dst, send_sem=send, recv_sem=recv,
            device_id=device, device_id_type=MESH,
        )

    col_p = pl.multiple_of(o * half, half)
    col_m = pl.multiple_of(c * half, half)
    col_x = pl.multiple_of(x * xblock + c * xhalf, xhalf)

    def local(src, dst, sem):
        return pltpu.make_async_copy(src, dst, load_sem.at[sem])

    load_ah = local(act_help_h, ah_v, 0)
    load_hc = local(help_count_h, help_count, 1)
    load_hot = local(hot_h, hot, 2)
    load_sc = local(scales_h, scales, 3)
    load_wp = local(weight.at[:, pl.ds(col_p, half)], w_v.at[:, pl.ds(col_p, half)], 4)
    load_wm = local(weight.at[:, pl.ds(col_m, half)], w_v.at[:, pl.ds(col_m, half)], 5)
    load_ao = local(act_own_h, ao_v, 6)
    load_oc = local(own_count_h, own_count, 7)
    load_g = local(dy_help.at[:, pl.ds(col_m, half)], pairs_g.at[pl.ds(0, hrows)], 8)
    load_gd = local(dy_help.at[:, pl.ds(col_x, xhalf)], gd.at[c, x], 9)
    load_dyo = local(dy_own, dyo_v, 10)
    for load in (load_ah, load_hc, load_hot, load_sc, load_wp, load_wm):
        load.start()
    for load in (load_ao, load_oc, load_gd, load_g, load_dyo):
        load.start()

    barrier = pltpu.get_barrier_semaphore()

    def greet(device):
        pl.semaphore_signal(barrier, inc=1, device_id=device, device_id_type=MESH)

    def greet_plane(d):
        px, py = lax.rem(x + d, n), lax.rem(y + d, n)
        for pc in range(2):
            greet(at(px, y, pc, z))
            greet(at(x, py, pc, z))

    def greet_line(d):
        pz = lax.rem(z + d, nz)
        for pc in range(2):
            greet(at(x, y, pc, pz))

    greet(partner)
    loop(1, n, greet_plane)
    loop(1, nz, greet_line)

    load_ah.wait()
    load_hc.wait()
    live_help = lax.broadcasted_iota(jnp.int32, (hrows, ff), 0) < help_count[0]
    help_a = jnp.where(live_help, ah_v[...].astype(F32), 0.0).astype(BF16)
    pairs_a[pl.ds(0, hrows), :] = help_a
    ad[c, x] = help_a

    load_hot.wait()
    load_sc.wait()
    flag = jnp.where(hot[0] == e, 1.0, 0.0).astype(F32)

    def scaled(col_base, at_first, dest, i):
        t = lax.rem(at_first + nth(i, n), n)
        for k in range(2):
            tile = lax.div(col_base, LANES) + 2 * t + k
            col = pl.multiple_of(tile * LANES, LANES)
            for part in range(3):
                third = ff // 3
                span = pl.ds(part * third, third)
                scale = scales[lax.div(3 * z + part, 2), 0, tile]
                wide = w_v[span, pl.ds(col, LANES)].astype(F32) * scale
                deq[span, pl.ds(col, LANES)] = wide.astype(BF16)
                dest[2 * i + k, span, :] = (wide * flag).astype(BF16)

    groups = min(4, n)
    each = n // groups

    pl.semaphore_wait(barrier, 4 * (n - 1) + 2 * (nz - 1) + 1)

    def send_a(i):
        p = lax.rem(x + nth(i, n), n)
        remote(
            pairs_a.at[pl.ds(0, hrows)], ad.at[c, x], xa_s.at[p], xa_r.at[x], along_x(p)
        ).start()

    pair_g = remote(
        dy_help.at[:, pl.ds(col_p, half)], pairs_g.at[pl.ds(hrows, hrows)],
        pair_s.at[0], pair_r.at[0], partner,
    )
    pair_a = remote(
        pairs_a.at[pl.ds(0, hrows)], pairs_a.at[pl.ds(hrows, hrows)],
        pair_s.at[1], pair_r.at[1], partner,
    )
    loop(0, n - 1, send_a)

    load_wp.wait()

    def exchange(q):
        tiles = pl.ds(q * 2 * each, 2 * each)
        return remote(give.at[tiles], got.at[tiles], ex_s.at[q], ex_r.at[q], partner)

    def give_group(q):
        for j in range(each):
            scaled(col_p, first_p, give, q * each + j)
        exchange(q).start()

    loop(0, groups, give_group)
    load_wm.wait()
    loop(0, n, functools.partial(scaled, col_m, first, mine))

    for q in range(groups):
        exchange(q).wait_recv()

    def merge(i):
        tiles = pl.ds(2 * i, 2)
        mine[tiles] = mine[tiles] + got[tiles]

    loop(0, n - 1, merge)
    r1[first] = mine[pl.ds(2 * n - 2, 2)] + got[pl.ds(2 * n - 2, 2)]
    high = ff // tall

    def strip(h):
        return lax.div(h, high), pl.ds(pl.multiple_of(lax.rem(h, high) * tall, 16), tall)

    def send_first(j):
        h, i = lax.div(j, n - 1), lax.rem(j, n - 1)
        t = lax.rem(first + nth(i, n), n)
        k, span = strip(h)
        remote(
            mine.at[2 * i + k, span], r1.at[first, k, span], s1_s.at[t], s1_r.at[first, h],
            along_first(t),
        ).start()

    loop(0, parts * (n - 1), send_first)

    def send_g(i):
        p = lax.rem(x + nth(i, n), n)
        for pc in range(2):
            block = pl.ds(pl.multiple_of(p * xblock + pc * xhalf, xhalf), xhalf)
            remote(
                dy_help.at[:, block], gd.at[c, x], xg_s.at[2 * p + pc], xg_r.at[2 * x + c],
                at(p, y, pc, z),
            ).start()

    loop(0, n - 1, send_g)
    block_o = pl.ds(pl.multiple_of(x * xblock + o * xhalf, xhalf), xhalf)
    gd_pair = remote(
        dy_help.at[:, block_o], gd.at[c, x], xg_s.at[2 * x + o], xg_r.at[2 * x + c], partner
    )
    gd_pair.start()
    pair_g.start()
    pair_a.start()

    load_ao.wait()
    load_oc.wait()
    live_own = lax.broadcasted_iota(jnp.int32, (ff, rows), 1) < own_count[0]
    own_a[...] = jnp.where(live_own, ao_v[...].astype(F32), 0.0).T.astype(BF16)

    def own_partial(pz):
        block = pl.ds(pl.multiple_of(pz * zblock, zblock), zblock)
        return jnp.dot(own_a[...], deq[:, block], preferred_element_type=F32).astype(BF16)

    def send_z(i):
        pz = lax.rem(z + nth(i, nz), nz)
        yp[pz] = own_partial(pz)
        remote(yp.at[pz], ry.at[z], z_s.at[pz], z_r.at[z], at(x, y, c, pz)).start()

    loop(0, nz - 1, send_z)
    ry[z] = own_partial(z)

    def wait_a(d):
        p = lax.rem(x + d, n)
        remote(ad.at[c, p], ad.at[c, p], xa_s.at[p], xa_r.at[p], along_x(p)).wait_recv()

    loop(1, n, wait_a)
    forward_a = remote(ad.at[c], ad.at[c], fa_s.at[0], fa_r.at[0], partner)
    forward_a.start()

    load_dyo.wait()
    kblock = 512

    def dact_step(j, total):
        block = pl.ds(pl.multiple_of(j * kblock, kblock), kblock)
        return total + lax.dot_general(
            deq[:, block], dyo_v[:, block], NT, preferred_element_type=F32
        )

    total = lax.fori_loop(0, depth // kblock, dact_step, jnp.zeros((ff, rows), F32))
    dact_own[...] = jnp.where(live_own, total, 0.0).astype(BF16)

    def place(s):
        return lax.div(s, per), pl.ds(pl.multiple_of(lax.rem(s, per) * chunk, 16), chunk)

    def spot(s):
        k, span = place(s)
        return wf.at[2 * first + k, span]

    def send_last(s):
        there = spot(s)

        def send(i):
            p = lax.rem(first + nth(i, n), n)
            remote(there, there, s4_s.at[p], s4_r.at[first], along_first(p)).start()

        loop(0, n - 1, send)

    def reduce_part(h):
        k, span = strip(h)

        def wait_first(d):
            p = lax.rem(first + d, n)
            there = r1.at[p, k, span]
            remote(there, there, s1_s.at[p], s1_r.at[p, h], along_first(p)).wait_recv()

        loop(1, n, wait_first)
        piece = r1[0, k, span, :].astype(F32)
        for p in range(1, n):
            piece = piece + r1[p, k, span, :].astype(F32)
        s2[k, span, :] = piece.astype(BF16)
        for j in range(both):
            s = both * h + j
            pk, pspan = place(s)

            @pl.when(s != second)
            def _():
                remote(
                    s2.at[pk, pspan], r2.at[second], s2_s.at[s], s2_r.at[second],
                    along_second(s),
                ).start()

            @pl.when(s == second)
            def _():
                r2[second] = piece[j * chunk : (j + 1) * chunk].astype(BF16)

    def reduce_mine():
        def wait_second(d):
            p = lax.rem(second + d, n)
            remote(r2.at[p], r2.at[p], s2_s.at[p], s2_r.at[p], along_second(p)).wait_recv()

        loop(1, n, wait_second)
        piece = r2[0].astype(F32)
        for p in range(1, n):
            piece = piece + r2[p].astype(F32)
        there = spot(second)
        there[...] = piece.astype(BF16)

        def send_third(i):
            p = lax.rem(second + nth(i, n), n)
            remote(there, there, s3_s.at[p], s3_r.at[second], along_second(p)).start()

        loop(0, n - 1, send_third)
        send_last(second)

    def pass_on(s):
        @pl.when(s != second)
        def _():
            there = spot(s)
            remote(there, there, s3_s.at[s], s3_r.at[s], along_second(s)).wait_recv()
            send_last(s)

    def stage(i):
        pl.when(i < parts)(lambda: reduce_part(i))
        pl.when(lax.div(second, both) == i - 2)(reduce_mine)

        @pl.when(i >= 4)
        def _():
            for j in range(both):
                pass_on(both * (i - 4) + j)

    loop(0, parts + 2, stage)

    load_gd.wait()
    forward_a.wait_recv()

    def wait_g(d):
        p = lax.rem(x + d, n)
        for pc in range(2):
            there = gd.at[pc, p]
            remote(there, there, xg_s.at[0], xg_r.at[2 * p + pc], at(p, y, pc, z)).wait_recv()

    loop(1, n, wait_g)
    there = gd.at[o, x]
    remote(there, there, xg_s.at[0], xg_r.at[2 * x + o], partner).wait_recv()
    dw[...] = lax.dot_general(
        gd[...].reshape(2 * n * hrows, xhalf), ad[...].reshape(2 * n * hrows, ff), TN,
        preferred_element_type=F32,
    )
    shared = n // 2

    def each_owner(body):
        def one(i):
            p = c * shared + lax.rem(y + lax.div(i, 2), shared)
            pc = lax.rem(i, 2)
            slot = 2 * lax.rem(y + lax.div(i, 2), shared) + pc
            part = dw.at[pl.ds(pl.multiple_of(slot * cols, cols), cols)]
            copy = remote(part, rd.at[y], dw_s.at[slot], dw_r.at[y], at(x, p, pc, z))
            body(copy, part, (p == y) & (pc == c))

        loop(0, n, one)

    def send_dw(copy, part, own):
        pl.when(jnp.logical_not(own))(copy.start)

        @pl.when(own)
        def _():
            rd[y] = part[...]

    each_owner(send_dw)

    loop(parts + 2, parts + 4, stage)

    def wait_z(d):
        p = lax.rem(z + d, nz)
        remote(ry.at[p], ry.at[p], z_s.at[p], z_r.at[p], at(x, y, c, p)).wait_recv()

    loop(1, nz, wait_z)

    def sum_z(i):
        span = pl.ds(pl.multiple_of(i * 16, 16), 16)
        piece = ry[0, span, :].astype(F32)
        for p in range(1, nz):
            piece = piece + ry[p, span, :].astype(F32)
        y_own[span, :] = piece.astype(BF16)

    loop(0, rows // 16, sum_z)

    load_g.wait()
    pair_g.wait_recv()
    pair_a.wait_recv()
    blocks = half // zblock
    tiles_per = zblock // LANES

    def wait_fourth(p):
        there = wf.at[pl.ds(2 * p, 2)]
        remote(there, there, s4_s.at[p], s4_r.at[p], along_first(p)).wait_recv()

    da = jnp.zeros((2 * hrows, ff), F32)
    for m in range(blocks):
        pz = c * blocks + m
        for p in range(m * tiles_per // 2, (m + 1) * tiles_per // 2):
            pl.when(first != p)(functools.partial(wait_fourth, p))
        block = jnp.concatenate([wf[m * tiles_per + j] for j in range(tiles_per)], axis=1)
        out = jnp.dot(pairs_a[...], block, preferred_element_type=F32).astype(BF16)
        ys[m] = out.reshape(2, hrows, zblock)
        remote(
            ys.at[m, 1], ryh.at[z], yh_s.at[2 * m + 1], yh_r.at[z], at(x, y, o, pz)
        ).start()

        @pl.when(pz != z)
        def _():
            remote(
                ys.at[m, 0], ryh.at[z], yh_s.at[2 * m], yh_r.at[z], at(x, y, c, pz)
            ).start()

        @pl.when(pz == z)
        def _():
            ryh[z] = ys[m, 0]

        da = da + lax.dot_general(
            pairs_g[:, m * zblock : (m + 1) * zblock], block, NT, preferred_element_type=F32
        )
    da_give[...] = da[hrows:]
    da_copy = remote(da_give, da_got, da_s.at[0], da_r.at[0], partner)
    da_copy.start()

    owner = lax.div(y, shared)

    def wait_dw(p):
        @pl.when((p != y) | (owner != c))
        def _():
            there = rd.at[p]
            remote(there, there, dw_s.at[0], dw_r.at[p], at(x, p, owner, z)).wait_recv()

    loop(0, n, wait_dw)
    total = rd[0]
    for p in range(1, n):
        total = total + rd[p]
    hot_grad[...] = total

    source = lax.div(z, blocks)

    def wait_yh(p):
        @pl.when((p != z) | (source != c))
        def _():
            remote(
                ryh.at[p], ryh.at[p], yh_s.at[0], yh_r.at[p], at(x, y, source, p)
            ).wait_recv()

    da_copy.wait_recv()
    dact_help[...] = jnp.where(live_help, da[:hrows] + da_got[...], 0.0).astype(BF16)

    loop(0, nz, wait_yh)
    piece = ryh[0].astype(F32)
    for p in range(1, nz):
        piece = piece + ryh[p].astype(F32)
    y_help[...] = piece.astype(BF16)

    for copy in (pair_a, pair_g, gd_pair, forward_a, da_copy):
        copy.wait_send()

    def drain_exchange(q):
        exchange(q).wait_send()

    loop(0, groups, drain_exchange)
    mine_spot = spot(second)

    def drain_plane(d):
        px, pf, ps = (lax.rem(v + d, n) for v in (x, first, second))
        for pc in range(2):
            there = gd.at[c, px]
            remote(there, there, xg_s.at[2 * px + pc], xg_r.at[0], at(px, y, pc, z)).wait_send()
        there = ad.at[c, px]
        remote(there, there, xa_s.at[px], xa_r.at[px], along_x(px)).wait_send()
        remote(r1.at[pf], r1.at[pf], s1_s.at[pf], s1_r.at[pf, 0], along_first(pf)).wait_send()
        remote(r2.at[ps], r2.at[ps], s2_s.at[ps], s2_r.at[ps], along_second(ps)).wait_send()
        remote(mine_spot, mine_spot, s3_s.at[ps], s3_r.at[ps], along_second(ps)).wait_send()
        there = wf.at[pl.ds(2 * first, 2)]
        remote(there, there, s4_s.at[pf], s4_r.at[pf], along_first(pf)).wait_send()

    loop(1, n, drain_plane)
    each_owner(lambda copy, part, own: pl.when(jnp.logical_not(own))(copy.wait_send))

    def drain_line(d):
        p = lax.rem(z + d, nz)
        remote(ry.at[p], ry.at[p], z_s.at[p], z_r.at[p], at(x, y, c, p)).wait_send()

    loop(1, nz, drain_line)
    for m in range(blocks):
        pz = c * blocks + m
        remote(
            ys.at[m, 1], ryh.at[z], yh_s.at[2 * m + 1], yh_r.at[z], at(x, y, o, pz)
        ).wait_send()

        @pl.when(pz != z)
        def _():
            remote(
                ys.at[m, 0], ryh.at[z], yh_s.at[2 * m], yh_r.at[z], at(x, y, c, pz)
            ).wait_send()


def finish(
    own_count, act, dy, y_in, da_in, yh_in, dah_in, hg_in, grad, y_out, da_out, yh_out, dah_out,
    hg_out,
):
    live = lax.broadcasted_iota(jnp.int32, act.shape, 1) < own_count[0]
    rows = jnp.where(live, act[...].astype(F32), 0.0).astype(BF16)
    grad[...] = jnp.dot(rows, dy[...], preferred_element_type=F32).astype(BF16)

    @pl.when(pl.program_id(0) == 0)
    def _():
        y_out[...] = y_in[...]
        da_out[...] = da_in[...]
        yh_out[...] = yh_in[...]
        dah_out[...] = dah_in[...]
        hg_out[...] = hg_in[...]


def solution(mesh):
    nz = mesh.shape["hidden"]
    n = 1
    while 2 * n * n < mesh.shape["expert"]:
        n += 1

    def body(weight, scales, act_own, dy_own, own_count, act_help, dy_help, help_count, hot):
        ff, depth = weight.shape[1:]
        rows, hrows = act_own.shape[1], act_help.shape[1]
        half, zblock, xblock = depth // 2, depth // nz, depth // n
        cols, chunk = xblock // (2 * n), 2 * ff // n
        tiles = half // LANES
        groups = min(4, n)
        blocks = half // zblock
        vmem = pltpu.VMEM
        dma = pltpu.SemaphoreType.DMA
        smem = pl.BlockSpec(memory_space=pltpu.SMEM)
        near = pl.BlockSpec(memory_space=pltpu.VMEM)
        far = pl.BlockSpec(memory_space=pl.ANY)
        act_t = jnp.swapaxes(act_own, 1, 2)[0]
        mid = (
            jax.ShapeDtypeStruct((rows, zblock), BF16),
            jax.ShapeDtypeStruct((ff, rows), BF16),
            jax.ShapeDtypeStruct((hrows, zblock), BF16),
            jax.ShapeDtypeStruct((hrows, ff), BF16),
            jax.ShapeDtypeStruct((cols, ff), F32),
        )
        outs = pl.pallas_call(
            functools.partial(kernel, (n, nz, ff, rows, hrows, depth)),
            out_shape=mid,
            in_specs=[pl.BlockSpec(memory_space=pltpu.HBM)] * 4 + [far] * 5,
            out_specs=(near,) * 5,
            scratch_shapes=[
                pltpu.SMEM((1,), jnp.int32),
                pltpu.SMEM((1,), jnp.int32),
                pltpu.SMEM((1,), jnp.int32),
                pltpu.SMEM((scales.shape[1], 1, scales.shape[2]), F32),
                vmem((ff, rows), BF16),
                vmem((hrows, ff), BF16),
                vmem((ff, depth), BF16),
                vmem((rows, depth), BF16),
                vmem((ff, depth), BF16),
                vmem((rows, ff), BF16),
                vmem((2 * hrows, ff), BF16),
                vmem((2 * hrows, half), BF16),
                vmem((tiles, ff, LANES), BF16),
                vmem((tiles, ff, LANES), BF16),
                vmem((tiles, ff, LANES), BF16),
                vmem((n, 2, ff, LANES), BF16),
                vmem((2, ff, LANES), BF16),
                vmem((n, chunk, LANES), BF16),
                vmem((tiles, ff, LANES), BF16),
                vmem((nz, rows, zblock), BF16),
                vmem((nz, rows, zblock), BF16),
                vmem((2, n, hrows, xblock // 2), BF16),
                vmem((2, n, hrows, ff), BF16),
                vmem((xblock // 2, ff), F32),
                vmem((n, cols, ff), F32),
                vmem((blocks, 2, hrows, zblock), BF16),
                vmem((nz, hrows, zblock), BF16),
                vmem((hrows, ff), F32),
                vmem((hrows, ff), F32),
                dma((11,)),
                dma((groups,)), dma((groups,)),
                dma((2,)), dma((2,)),
                dma((n,)), dma((n,)),
                dma((2 * n,)), dma((2 * n,)),
                dma((1,)), dma((1,)),
                dma((nz,)), dma((nz,)),
                dma((n,)), dma((n, n)),
                dma((n,)), dma((n,)),
                dma((n,)), dma((n,)),
                dma((n,)), dma((n,)),
                dma((n,)), dma((n,)),
                dma((2 * blocks,)), dma((nz,)),
                dma((1,)), dma((1,)),
            ],
            compiler_params=pltpu.CompilerParams(collective_id=0, has_side_effects=True),
            name="moe_step",
        )(
            hot, own_count, help_count, jnp.swapaxes(scales, 0, 1), act_t, act_help[0],
            weight[0], dy_own[0], dy_help[0],
        )
        steps = 4
        whole = lambda a: pl.BlockSpec(a.shape, lambda i: (0,) * len(a.shape))
        done = pl.pallas_call(
            finish,
            grid=(steps,),
            out_shape=(jax.ShapeDtypeStruct((ff, depth), BF16), *mid),
            in_specs=[
                smem, whole(act_t), pl.BlockSpec((rows, depth // steps), lambda i: (0, i)),
                *(whole(a) for a in mid),
            ],
            out_specs=(
                pl.BlockSpec((ff, depth // steps), lambda i: (0, i)), *(whole(a) for a in mid)
            ),
            name="finish",
        )(own_count, act_t, dy_own[0], *outs)
        own_grad, own, dact_own, helped, dact_help, hot_grad = done
        dact_own = jnp.swapaxes(dact_own[None], 1, 2)
        return own[None], dact_own, own_grad[None], helped[None], dact_help[None], hot_grad.T

    return jax.shard_map(
        body,
        mesh=mesh,
        in_specs=(
            P("expert", "hidden", None),
            P("expert", None, None),
            P("expert", None, "hidden"),
            P("expert", None, None),
            P("expert"),
            P("expert", None, "hidden"),
            P("expert", None, None),
            P("expert"),
            P(),
        ),
        out_specs=(
            P("expert", None, "hidden"),
            P("expert", None, "hidden"),
            P("expert", "hidden", None),
            P("expert", None, "hidden"),
            P("expert", None, "hidden"),
            P("hidden", "expert"),
        ),
        check_vma=False,
    )
```

time: 94.7 us -> 75 us (0.79)
  the two profiles are of different devices: /device:TPU:10 before, /device:TPU:1 now
where the time goes in v2:
time: 75 us; the launch traced here: 74.8 us
  Pallas kernels  72.2 us (96%)
  between operations  2.58 us (3%)
    pallas_call x1, Pallas kernels, body(): pl.pallas_call(functools.partial(kernel, (n, nz, ff, rows, hrows, depth))...  68.1 us
    pallas_call x1, Pallas kernels, body(): pl.pallas_call(finish, grid=(steps,), out_shape=(jax.ShapeDtypeStruct((ff...  4.06 us

profile of v2, /device:TPU:1, one launch (start us, length us, event | category | flops | bytes accessed | tf_op | source)
XLA Modules:
  0.0 74.8 jit_solution(14973193247861571746)
XLA Ops:
  2.6 68.1 %moe_step.1 = (bf16[128,512]{1,0:T(8,128)(2,1)}, bf16[192,128]{1,0:T(8,128)(2,1)}, bf16[32,512]{1,0:T(8,128)(2,1)}, bf16[32,192]{1,0:T(8,128)(2,1)}, f32[32,192]{1,0:T(8,128)}) custom-call(s32[1]{0:T(128)S(6)} %copy.17.hot_h, s32[1]{0:T(128)S(6)} %copy.15.own_count_h.own_count, s32[1]{0:T(128)S(6)} %copy.16.help_count_h, f32[12,1,32]{2,1,0:T(1,128)} %bitcast.23, ...), custom_call_target="tpu_custom_call" | custom-call | tf_op jit(solution)/shard_map/moe_step/pallas_call | solution.py:555
  70.7 4.1 %finish.1 = (bf16[192,4096]{1,0:T(8,128)(2,1)}, bf16[128,512]{1,0:T(8,128)(2,1)}, bf16[192,128]{1,0:T(8,128)(2,1)}, bf16[32,512]{1,0:T(8,128)(2,1)}, bf16[32,192]{1,0:T(8,128)(2,1)}, /*index=5*/f32[32,192]{1,0:T(8,128)}) custom-call(s32[1]{0:T(128)S(6)} %copy.15.own_count_h.own_count, bf16[192,128]{1,0:T(8,128)(2,1)} %bitcast.21, ...), custom_call_target="tpu_custom_call" | custom-call | tf_op jit(solution)/shard_map/finish/pallas_call | solution.py:613

commit v3 on v2

v3 whole, which is shorter than its diff:
```python
import functools

import jax
import jax.numpy as jnp
from jax import lax
from jax.experimental import pallas as pl
from jax.experimental.pallas import tpu as pltpu
from jax.sharding import PartitionSpec as P

MESH = pl.DeviceIdType.MESH
BF16 = jnp.bfloat16
F32 = jnp.float32
LANES = 128
NT = (((1,), (1,)), ((), ()))
TN = (((0,), (0,)), ((), ()))


def kernel(
    cfg,
    hot_h, own_count_h, help_count_h, scales_h, act_own_h, act_help_h, weight, dy_own, dy_help,
    y_own, dact_own, y_help, dact_help, hot_grad,
    hot, own_count, help_count, scales, ao_v, ah_v,
    w_v, dyo_v, deq, own_a, a8, g8, mine, give, got, r1, s2, r2, wb,
    yp, ry, dw, rd, ys, ryh, da_give, da_got,
    load_sem, ex_s, ex_r, xa_s, xa_r, xg_s, xg_r, z_s, z_r,
    s1_s, s1_r, s2_s, s2_r, s4_s, s4_r, dw_s, dw_r, yh_s, yh_r, da_s, da_r,
):
    n, nz, ff, rows, hrows, depth = cfg
    half = depth // 2
    zblock = depth // nz
    wide = depth // 8
    spread = 8 // nz
    owners = 2 * n * n // 8
    cols = wide // owners
    parts = 4
    tall = ff // 2
    e, z = lax.axis_index("expert"), lax.axis_index("hidden")
    x, y, c = lax.div(e, 2 * n), lax.rem(lax.div(e, 2), n), lax.rem(e, 2)
    o = 1 - c

    def at(px, py, pc, pz):
        return ((px * n + py) * 2 + pc, pz)

    first = o * x + c * y
    second = o * y + c * x
    first_p = o * y + c * x

    def along_first(p):
        return at(o * p + c * x, o * y + c * p, c, z)

    def along_second(p):
        return at(o * x + c * p, o * p + c * y, c, z)

    def mate(j, pz):
        return at(
            x - lax.rem(x, 2) + lax.rem(lax.div(j, 2), 2), y - lax.rem(y, 2) + lax.rem(j, 2),
            lax.div(j, 4), pz,
        )

    def block_of(j):
        jc, jx, jy = lax.div(j, 4), lax.rem(lax.div(j, 2), 2), lax.rem(j, 2)
        return 4 * jc + (1 - jc) * (2 * jx + jy) + jc * (2 * jy + jx)

    me = 4 * c + 2 * lax.rem(x, 2) + lax.rem(y, 2)
    mb = block_of(me)

    def holder(b, i):
        f = 2 * lax.div(i, n // 2) + lax.rem(lax.div(b, 2), 2)
        s = 2 * lax.rem(i, n // 2) + lax.rem(b, 2)
        bc = lax.div(b, 4)
        return at((1 - bc) * f + bc * s, (1 - bc) * s + bc * f, bc, z)

    seat = lax.div(first, 2) * (n // 2) + lax.div(second, 2)

    partner = at(x, y, o, z)

    def loop(low, high, body):
        def step(i, carry):
            body(i)
            return carry

        lax.fori_loop(low, high, step, 0)

    def nth(i, count):
        turn = jnp.where(lax.rem(i, 2) == 0, lax.div(i, 2) + 1, count - lax.div(i + 1, 2))
        return jnp.where(i == count - 1, 0, turn)

    def remote(src, dst, send, recv, device):
        return pltpu.make_async_remote_copy(
            src_ref=src, dst_ref=dst, send_sem=send, recv_sem=recv,
            device_id=device, device_id_type=MESH,
        )

    col_p = pl.multiple_of(o * half, half)
    col_m = pl.multiple_of(c * half, half)
    col_b = pl.multiple_of(mb * wide, wide)

    def local(src, dst, sem):
        return pltpu.make_async_copy(src, dst, load_sem.at[sem])

    load_ah = local(act_help_h, ah_v, 0)
    load_hc = local(help_count_h, help_count, 1)
    load_hot = local(hot_h, hot, 2)
    load_sc = local(scales_h, scales, 3)
    load_wp = local(weight.at[:, pl.ds(col_p, half)], w_v.at[:, pl.ds(col_p, half)], 4)
    load_wm = local(weight.at[:, pl.ds(col_m, half)], w_v.at[:, pl.ds(col_m, half)], 5)
    load_ao = local(act_own_h, ao_v, 6)
    load_oc = local(own_count_h, own_count, 7)
    load_g = local(dy_help.at[:, pl.ds(col_b, wide)], g8.at[me], 8)
    load_dyo = local(dy_own, dyo_v, 9)
    for load in (load_ah, load_hc, load_hot, load_sc, load_wp, load_wm):
        load.start()
    for load in (load_g, load_ao, load_oc, load_dyo):
        load.start()

    barrier = pltpu.get_barrier_semaphore()

    def greet(device):
        pl.semaphore_signal(barrier, inc=1, device_id=device, device_id_type=MESH)

    def greet_lines(d):
        greet(along_first(lax.rem(first + d, n)))
        greet(along_second(lax.rem(second + d, n)))

    def greet_z(d):
        greet(at(x, y, c, lax.rem(z + d, nz)))

    def greet_mate(d):
        greet(mate(lax.rem(me + d, 8), z))

    my_b = lax.div(e, owners)
    in_b = (mb == my_b).astype(jnp.int32)

    def sender(i):
        b = z * spread + lax.rem(i, spread)
        bc = lax.div(b, 4)
        b1, b0 = lax.rem(lax.div(b, 2), 2), lax.rem(b, 2)
        return 4 * bc + (1 - bc) * (2 * b1 + b0) + bc * (2 * b0 + b1), lax.div(i, spread)

    loop(1, n, greet_lines)
    loop(1, nz, greet_z)
    loop(1, 8, greet_mate)

    load_ah.wait()
    load_hc.wait()
    live_help = lax.broadcasted_iota(jnp.int32, (hrows, ff), 0) < help_count[0]
    help_a = jnp.where(live_help, ah_v[...].astype(F32), 0.0).astype(BF16)
    a8[me] = help_a

    load_hot.wait()
    load_sc.wait()
    flag = jnp.where(hot[0] == e, 1.0, 0.0).astype(F32)

    def tile_of(base, t):
        b = 2 * lax.rem(t, 2) + lax.rem(lax.div(t, 2), 2)
        return base + b * (wide // LANES) + 2 * lax.div(t, 4)

    def scaled(col_base, at_first, dest, i):
        t = lax.rem(at_first + nth(i, n), n)
        for k in range(2):
            tile = tile_of(lax.div(col_base, LANES), t) + k
            col = pl.multiple_of(tile * LANES, LANES)
            for part in range(3):
                third = ff // 3
                span = pl.ds(part * third, third)
                scale = scales[lax.div(3 * z + part, 2), 0, tile]
                wide = w_v[span, pl.ds(col, LANES)].astype(F32) * scale
                deq[span, pl.ds(col, LANES)] = wide.astype(BF16)
                dest[2 * i + k, span, :] = (wide * flag).astype(BF16)

    groups = min(4, n)
    each = n // groups

    pl.semaphore_wait(barrier, 2 * (n - 1) + (nz - 1) + 7)

    def send_mate(d):
        j = lax.rem(me + d, 8)
        remote(a8.at[me], a8.at[me], xa_s.at[j], xa_r.at[me], mate(j, z)).start()
        block = pl.ds(pl.multiple_of(block_of(j) * wide, wide), wide)
        remote(dy_help.at[:, block], g8.at[me], xg_s.at[j], xg_r.at[me], mate(j, z)).start()

    loop(1, 8, send_mate)

    load_wp.wait()

    def exchange(q):
        tiles = pl.ds(q * 2 * each, 2 * each)
        return remote(give.at[tiles], got.at[tiles], ex_s.at[q], ex_r.at[q], partner)

    def give_group(q):
        for j in range(each):
            scaled(col_p, first_p, give, q * each + j)
        exchange(q).start()

    loop(0, groups, give_group)
    load_wm.wait()
    loop(0, n, functools.partial(scaled, col_m, first, mine))

    for q in range(groups):
        exchange(q).wait_recv()

    def merge(i):
        tiles = pl.ds(2 * i, 2)
        mine[tiles] = mine[tiles] + got[tiles]

    loop(0, n - 1, merge)
    r1[first] = mine[pl.ds(2 * n - 2, 2)] + got[pl.ds(2 * n - 2, 2)]
    high = 2

    def strip(h):
        return lax.div(h, high), pl.ds(pl.multiple_of(lax.rem(h, high) * tall, 16), tall)

    def send_first(j):
        h, i = lax.div(j, n - 1), lax.rem(j, n - 1)
        t = lax.rem(first + nth(i, n), n)
        k, span = strip(h)
        remote(
            mine.at[2 * i + k, span], r1.at[first, k, span], s1_s.at[t], s1_r.at[first, h],
            along_first(t),
        ).start()

    loop(0, parts * (n - 1), send_first)

    load_ao.wait()
    load_oc.wait()
    live_own = lax.broadcasted_iota(jnp.int32, (ff, rows), 1) < own_count[0]
    own_a[...] = jnp.where(live_own, ao_v[...].astype(F32), 0.0).T.astype(BF16)

    def own_partial(pz):
        block = pl.ds(pl.multiple_of(pz * zblock, zblock), zblock)
        return jnp.dot(own_a[...], deq[:, block], preferred_element_type=F32).astype(BF16)

    def send_z(i):
        pz = lax.rem(z + nth(i, nz), nz)
        yp[pz] = own_partial(pz)
        remote(yp.at[pz], ry.at[z], z_s.at[pz], z_r.at[z], at(x, y, c, pz)).start()

    loop(0, nz - 1, send_z)
    ry[z] = own_partial(z)

    load_dyo.wait()
    kblock = 512

    def dact_step(j, total):
        block = pl.ds(pl.multiple_of(j * kblock, kblock), kblock)
        return total + lax.dot_general(
            deq[:, block], dyo_v[:, block], NT, preferred_element_type=F32
        )

    total = lax.fori_loop(0, depth // kblock, dact_step, jnp.zeros((ff, rows), F32))
    dact_own[...] = jnp.where(live_own, total, 0.0).astype(BF16)

    parity = lax.rem(lax.div(first, 2), 2)
    keeps = parity == lax.rem(second, 2)
    u = lax.div(first, 4)

    def reduce_part(h):
        k, span = strip(h)

        def wait_first(d):
            p = lax.rem(first + d, n)
            there = r1.at[p, k, span]
            remote(there, there, s1_s.at[p], s1_r.at[p, h], along_first(p)).wait_recv()

        loop(1, n, wait_first)
        piece = r1[0, k, span, :].astype(F32)
        for p in range(1, n):
            piece = piece + r1[p, k, span, :].astype(F32)
        s2[k, span, :] = piece.astype(BF16)

        def send_second(i):
            p = lax.rem(2 * i + second - lax.rem(second, 2) + parity, n)

            @pl.when(p != second)
            def _():
                remote(
                    s2.at[k, span], r2.at[second, k, span], s2_s.at[p], s2_r.at[second, h],
                    along_second(p),
                ).start()

        loop(0, n // 2, send_second)

        @pl.when(keeps)
        def _():
            r2[second, k, span, :] = piece.astype(BF16)

    def keep_part(h):
        k, span = strip(h)

        def wait_second(d):
            p = lax.rem(second + d, n)
            there = r2.at[p, k, span]
            remote(there, there, s2_s.at[p], s2_r.at[p, h], along_second(p)).wait_recv()

        loop(1, n, wait_second)
        piece = r2[0, k, span, :].astype(F32)
        for p in range(1, n):
            piece = piece + r2[p, k, span, :].astype(F32)
        there = wb.at[u, k, span]
        there[...] = piece.astype(BF16)

        def send_last(i):
            p = lax.rem(first + 2 * i, n)
            remote(there, there, s4_s.at[p], s4_r.at[u], along_first(p)).start()

        loop(1, n // 2, send_last)

    def stage(i):
        pl.when(i < parts)(lambda: reduce_part(i))
        pl.when((i >= 2) & keeps)(lambda: keep_part(i - 2))

    loop(0, parts, stage)

    loop(parts, parts + 2, stage)

    load_g.wait()

    def wait_mate(d):
        j = lax.rem(me + d, 8)
        remote(a8.at[j], a8.at[j], xa_s.at[j], xa_r.at[j], mate(j, z)).wait_recv()
        remote(g8.at[j], g8.at[j], xg_s.at[j], xg_r.at[j], mate(j, z)).wait_recv()

    loop(1, 8, wait_mate)
    dw[...] = lax.dot_general(
        g8[...].reshape(8 * hrows, wide), a8[...].reshape(8 * hrows, ff), TN,
        preferred_element_type=F32,
    ).astype(BF16)

    def each_owner(body):
        def one(d):
            i = lax.rem(seat + d, owners)
            part = dw.at[pl.ds(pl.multiple_of(i * cols, cols), cols)]
            owner = mb * owners + i
            copy = remote(part, rd.at[seat], dw_s.at[i], dw_r.at[seat], (owner, z))
            body(copy, part, owner == e)

        loop(0, owners, one)

    def send_dw(copy, part, own):
        pl.when(jnp.logical_not(own))(copy.start)

        @pl.when(own)
        def _():
            rd[seat] = part[...]

    each_owner(send_dw)

    def wait_z(d):
        p = lax.rem(z + d, nz)
        remote(ry.at[p], ry.at[p], z_s.at[p], z_r.at[p], at(x, y, c, p)).wait_recv()

    loop(1, nz, wait_z)

    def sum_z(i):
        span = pl.ds(pl.multiple_of(i * 16, 16), 16)
        piece = ry[0, span, :].astype(F32)
        for p in range(1, nz):
            piece = piece + ry[p, span, :].astype(F32)
        y_own[span, :] = piece.astype(BF16)

    loop(0, rows // 16, sum_z)

    for i in range(n // 4):
        t = lax.rem(first, 2) + 2 * lax.rem(second, 2) + 4 * i

        @pl.when(t != first)
        def _():
            remote(wb.at[i], wb.at[i], s4_s.at[t], s4_r.at[i], along_first(t)).wait_recv()

    block = jnp.concatenate([wb[j // 2, j % 2] for j in range(n // 2)], axis=1)
    out = jnp.dot(a8[...].reshape(8 * hrows, ff), block, preferred_element_type=F32)
    ys[...] = out.astype(BF16).reshape(8, hrows, wide)
    pz = lax.div(mb, spread)
    sub = lax.rem(mb, spread)
    landing = pl.ds(pl.multiple_of(sub * wide, wide), wide)

    def helped(j):
        return remote(
            ys.at[j], ryh.at[z, :, landing], yh_s.at[j], yh_r.at[z, sub], mate(j, pz)
        )

    def send_helped(d):
        j = lax.rem(me + d, 8)
        own = (j == me) & (pz == z)
        pl.when(jnp.logical_not(own))(helped(j).start)

        @pl.when(own)
        def _():
            ryh[z, :, landing] = ys[j]

    loop(0, 8, send_helped)
    da = lax.dot_general(
        g8[...].reshape(8 * hrows, wide), block, NT, preferred_element_type=F32
    )
    da_give[...] = da.astype(BF16).reshape(8, hrows, ff)

    def da_copy(j):
        return remote(da_give.at[j], da_got.at[me], da_s.at[j], da_r.at[me], mate(j, z))

    loop(1, 8, lambda d: da_copy(lax.rem(me + d, 8)).start())
    da_got[me] = da_give[me]

    def wait_dw(i):
        @pl.when((i != seat) | (in_b == 0))
        def _():
            remote(rd.at[i], rd.at[i], dw_s.at[i], dw_r.at[i], holder(my_b, i)).wait_recv()

    loop(0, owners, wait_dw)
    total = rd[0].astype(F32)
    for p in range(1, owners):
        total = total + rd[p].astype(F32)
    hot_grad[...] = total

    def wait_da(d):
        j = lax.rem(me + d, 8)
        remote(da_got.at[j], da_got.at[j], da_s.at[j], da_r.at[j], mate(j, z)).wait_recv()

    loop(1, 8, wait_da)
    total = da_got[0].astype(F32)
    for j in range(1, 8):
        total = total + da_got[j].astype(F32)
    dact_help[...] = jnp.where(live_help, total, 0.0).astype(BF16)

    def wait_helped(i):
        j, p = sender(i)

        @pl.when((j != me) | (p != z))
        def _():
            s = lax.rem(i, spread)
            there = ryh.at[p, :, pl.ds(pl.multiple_of(s * wide, wide), wide)]
            remote(there, there, yh_s.at[0], yh_r.at[p, s], mate(j, p)).wait_recv()

    loop(0, 8, wait_helped)
    piece = ryh[0].astype(F32)
    for p in range(1, nz):
        piece = piece + ryh[p].astype(F32)
    y_help[...] = piece.astype(BF16)

    def drain_exchange(q):
        exchange(q).wait_send()

    loop(0, groups, drain_exchange)

    def drain_mate(d):
        j = lax.rem(me + d, 8)
        remote(a8.at[j], a8.at[j], xa_s.at[j], xa_r.at[j], mate(j, z)).wait_send()
        remote(g8.at[j], g8.at[j], xg_s.at[j], xg_r.at[j], mate(j, z)).wait_send()
        da_copy(j).wait_send()

    loop(1, 8, drain_mate)

    def drain_first(d):
        p = lax.rem(first + d, n)
        remote(r1.at[p], r1.at[p], s1_s.at[p], s1_r.at[p, 0], along_first(p)).wait_send()

    loop(1, n, drain_first)

    def drain_second(i):
        p = lax.rem(2 * i + second - lax.rem(second, 2) + parity, n)

        @pl.when(p != second)
        def _():
            remote(r2.at[p], r2.at[p], s2_s.at[p], s2_r.at[p, 0], along_second(p)).wait_send()

        @pl.when(keeps & (i > 0))
        def _():
            p = lax.rem(first + 2 * i, n)
            remote(wb.at[u], wb.at[u], s4_s.at[p], s4_r.at[u], along_first(p)).wait_send()

    loop(0, n // 2, drain_second)
    each_owner(lambda copy, part, own: pl.when(jnp.logical_not(own))(copy.wait_send))

    def drain_line(d):
        p = lax.rem(z + d, nz)
        remote(ry.at[p], ry.at[p], z_s.at[p], z_r.at[p], at(x, y, c, p)).wait_send()

    loop(1, nz, drain_line)

    def drain_helped(j):
        pl.when((j != me) | (pz != z))(helped(j).wait_send)

    loop(0, 8, drain_helped)


def finish(*refs):
    own_count, act, dy = refs[:3]
    mids, grad, outs = refs[3:8], refs[8], refs[9:14]
    act_v, dy_v, grad_v, held, sem = refs[14], refs[15], refs[16], refs[17:22], refs[22]
    steps = 4
    width = dy.shape[1] // steps

    def part(ref, j):
        return ref.at[:, pl.ds(j * width, width)]

    def copy(src, dst, i):
        return pltpu.make_async_copy(src, dst, sem.at[i])

    loads = [copy(act, act_v, 0)]
    loads += [copy(part(dy, j), part(dy_v, j), 1 + j) for j in range(steps)]
    takes = [copy(mids[i], held[i], 1 + steps + i) for i in range(5)]
    gives = [copy(held[i], outs[i], 6 + steps + i) for i in range(5)]
    stores = [copy(part(grad_v, j), part(grad, j), 11 + steps + j) for j in range(steps)]
    for load in loads + takes:
        load.start()
    loads[0].wait()
    live = lax.broadcasted_iota(jnp.int32, act.shape, 1) < own_count[0]
    rows = jnp.where(live, act_v[...].astype(F32), 0.0).astype(BF16)
    for j in range(steps):
        loads[1 + j].wait()
        span = pl.ds(j * width, width)
        grad_v[:, span] = jnp.dot(
            rows, dy_v[:, span], preferred_element_type=F32
        ).astype(BF16)
        stores[j].start()
    for take, give in zip(takes, gives):
        take.wait()
        give.start()
    for out in gives + stores:
        out.wait()


def solution(mesh):
    nz = mesh.shape["hidden"]
    n = 1
    while 2 * n * n < mesh.shape["expert"]:
        n += 1

    def body(weight, scales, act_own, dy_own, own_count, act_help, dy_help, help_count, hot):
        ff, depth = weight.shape[1:]
        rows, hrows = act_own.shape[1], act_help.shape[1]
        half, zblock, wide = depth // 2, depth // nz, depth // 8
        owners, cols = n * n // 4, depth // (2 * n * n)
        tiles = half // LANES
        groups = min(4, n)
        vmem = pltpu.VMEM
        dma = pltpu.SemaphoreType.DMA
        smem = pl.BlockSpec(memory_space=pltpu.SMEM)
        near = pl.BlockSpec(memory_space=pltpu.VMEM)
        far = pl.BlockSpec(memory_space=pl.ANY)
        act_t = jnp.swapaxes(act_own, 1, 2)[0]
        mid = (
            jax.ShapeDtypeStruct((rows, zblock), BF16),
            jax.ShapeDtypeStruct((ff, rows), BF16),
            jax.ShapeDtypeStruct((hrows, zblock), BF16),
            jax.ShapeDtypeStruct((hrows, ff), BF16),
            jax.ShapeDtypeStruct((cols, ff), F32),
        )
        outs = pl.pallas_call(
            functools.partial(kernel, (n, nz, ff, rows, hrows, depth)),
            out_shape=mid,
            in_specs=[pl.BlockSpec(memory_space=pltpu.HBM)] * 4 + [far] * 5,
            out_specs=(near,) * 5,
            scratch_shapes=[
                pltpu.SMEM((1,), jnp.int32),
                pltpu.SMEM((1,), jnp.int32),
                pltpu.SMEM((1,), jnp.int32),
                pltpu.SMEM((scales.shape[1], 1, scales.shape[2]), F32),
                vmem((ff, rows), BF16),
                vmem((hrows, ff), BF16),
                vmem((ff, depth), BF16),
                vmem((rows, depth), BF16),
                vmem((ff, depth), BF16),
                vmem((rows, ff), BF16),
                vmem((8, hrows, ff), BF16),
                vmem((8, hrows, wide), BF16),
                vmem((tiles, ff, LANES), BF16),
                vmem((tiles, ff, LANES), BF16),
                vmem((tiles, ff, LANES), BF16),
                vmem((n, 2, ff, LANES), BF16),
                vmem((2, ff, LANES), BF16),
                vmem((n, 2, ff, LANES), BF16),
                vmem((n // 4, 2, ff, LANES), BF16),
                vmem((nz, rows, zblock), BF16),
                vmem((nz, rows, zblock), BF16),
                vmem((wide, ff), BF16),
                vmem((owners, cols, ff), BF16),
                vmem((8, hrows, wide), BF16),
                vmem((nz, hrows, zblock), BF16),
                vmem((8, hrows, ff), BF16),
                vmem((8, hrows, ff), BF16),
                dma((10,)),
                dma((groups,)), dma((groups,)),
                dma((8,)), dma((8,)),
                dma((8,)), dma((8,)),
                dma((nz,)), dma((nz,)),
                dma((n,)), dma((n, 4)),
                dma((n,)), dma((n, 4)),
                dma((n,)), dma((n // 4,)),
                dma((owners,)), dma((owners,)),
                dma((8,)), dma((nz, 8 // nz)),
                dma((8,)), dma((8,)),
            ],
            compiler_params=pltpu.CompilerParams(collective_id=0, has_side_effects=True),
            name="moe_step",
        )(
            hot, own_count, help_count, jnp.swapaxes(scales, 0, 1), act_t, act_help[0],
            weight[0], dy_own[0], dy_help[0],
        )
        done = pl.pallas_call(
            finish,
            out_shape=(jax.ShapeDtypeStruct((ff, depth), BF16), *mid),
            in_specs=[smem] + [far] * 7,
            out_specs=(far,) * 6,
            scratch_shapes=[
                vmem((ff, rows), BF16), vmem((rows, depth), BF16), vmem((ff, depth), BF16),
                *(vmem(a.shape, a.dtype) for a in mid), dma((19,)),
            ],
            name="finish",
        )(own_count, act_t, dy_own[0], *outs)
        own_grad, own, dact_own, helped, dact_help, hot_grad = done
        dact_own = jnp.swapaxes(dact_own[None], 1, 2)
        return own[None], dact_own, own_grad[None], helped[None], dact_help[None], hot_grad.T

    return jax.shard_map(
        body,
        mesh=mesh,
        in_specs=(
            P("expert", "hidden", None),
            P("expert", None, None),
            P("expert", None, "hidden"),
            P("expert", None, None),
            P("expert"),
            P("expert", None, "hidden"),
            P("expert", None, None),
            P("expert"),
            P(),
        ),
        out_specs=(
            P("expert", None, "hidden"),
            P("expert", None, "hidden"),
            P("expert", "hidden", None),
            P("expert", None, "hidden"),
            P("expert", None, "hidden"),
            P("hidden", "expert"),
        ),
        check_vma=False,
    )
```

time: 75 us -> 72 us (0.960)
  Pallas kernels: 72.2 us -> 69.2 us
    pallas_call x1, Pallas kernels: 68.1 us -> 66.2 us  [body(): pl.pallas_call(functools.partial(kernel, (n, nz, ff, rows, hrows, depth))...]
    pallas_call x1, Pallas kernels: 4.06 us -> 2.98 us  [body(): pl.pallas_call(finish, out_shape=(jax.ShapeDtypeStruct((ff, depth), BF16)...]
where the time goes in v3:
time: 72 us; the launch traced here: 71.8 us
  Pallas kernels  69.2 us (96%)
  between operations  2.58 us (4%)
    pallas_call x1, Pallas kernels, body(): pl.pallas_call(functools.partial(kernel, (n, nz, ff, rows, hrows, depth))...  66.2 us
    pallas_call x1, Pallas kernels, body(): pl.pallas_call(finish, out_shape=(jax.ShapeDtypeStruct((ff, depth), BF16)...  2.98 us

profile of v3, /device:TPU:1, one launch (start us, length us, event | category | flops | bytes accessed | tf_op | source)
XLA Modules:
  0.0 71.8 jit_solution(9799950861362991138)
XLA Ops:
  2.6 66.2 %moe_step.1 = (bf16[128,512]{1,0:T(8,128)(2,1)}, bf16[192,128]{1,0:T(8,128)(2,1)}, bf16[32,512]{1,0:T(8,128)(2,1)}, bf16[32,192]{1,0:T(8,128)(2,1)}, f32[32,192]{1,0:T(8,128)}) custom-call(s32[1]{0:T(128)S(6)} %copy.17.hot_h, s32[1]{0:T(128)S(6)} %copy.15.own_count_h.refs_0_, s32[1]{0:T(128)S(6)} %copy.16.help_count_h, f32[12,1,32]{2,1,0:T(1,128)} %bitcast.23, ...), custom_call_target="tpu_custom_call" | custom-call | tf_op jit(solution)/shard_map/moe_step/pallas_call | solution.py:548
  68.8 3.0 %finish.1 = (bf16[192,4096]{1,0:T(8,128)(2,1)}, bf16[128,512]{1,0:T(8,128)(2,1)}, bf16[192,128]{1,0:T(8,128)(2,1)}, bf16[32,512]{1,0:T(8,128)(2,1)}, bf16[32,192]{1,0:T(8,128)(2,1)}, /*index=5*/f32[32,192]{1,0:T(8,128)}) custom-call(s32[1]{0:T(128)S(6)} %copy.15.own_count_h.refs_0_, bf16[192,128]{1,0:T(8,128)(2,1)} %bitcast.21, bf16[128,4096]{1,0:T(8,128)(2,1)} %bitcast.17, ...), custom_call_target="tpu_custom_call" | custom-call | tf_op jit(solution)/shard_map/finish/pallas_call | solution.py:599

commit v4 on v3

--- a/solution.py
+++ b/solution.py
@@ -155,21 +155,25 @@
         b = 2 * lax.rem(t, 2) + lax.rem(lax.div(t, 2), 2)
         return base + b * (wide // LANES) + 2 * lax.div(t, 4)
 
-    def scaled(col_base, at_first, dest, i):
-        t = lax.rem(at_first + nth(i, n), n)
-        for k in range(2):
-            tile = tile_of(lax.div(col_base, LANES), t) + k
+    third = ff // 3
+    runs = (
+        ((0, third, 0), (third, tall - third, 1)),
+        ((tall, 2 * third - tall, 1), (2 * third, third, 2)),
+    )
+
+    def scaled(h, col_base, at_first, dest):
+        def one(i):
+            t = lax.rem(at_first + nth(i, n), n)
+            tile = tile_of(lax.div(col_base, LANES), t) + h // 2
             col = pl.multiple_of(tile * LANES, LANES)
-            for part in range(3):
-                third = ff // 3
-                span = pl.ds(part * third, third)
+            for start, size, part in runs[h % 2]:
+                span = pl.ds(start, size)
                 scale = scales[lax.div(3 * z + part, 2), 0, tile]
                 wide = w_v[span, pl.ds(col, LANES)].astype(F32) * scale
                 deq[span, pl.ds(col, LANES)] = wide.astype(BF16)
-                dest[2 * i + k, span, :] = (wide * flag).astype(BF16)
-
-    groups = min(4, n)
-    each = n // groups
+                dest[i, h // 2, span, :] = (wide * flag).astype(BF16)
+
+        loop(0, n, one)
 
     pl.semaphore_wait(barrier, 2 * (n - 1) + (nz - 1) + 7)
 
@@ -183,43 +187,33 @@
 
     load_wp.wait()
 
-    def exchange(q):
-        tiles = pl.ds(q * 2 * each, 2 * each)
-        return remote(give.at[tiles], got.at[tiles], ex_s.at[q], ex_r.at[q], partner)
-
-    def give_group(q):
-        for j in range(each):
-            scaled(col_p, first_p, give, q * each + j)
-        exchange(q).start()
-
-    loop(0, groups, give_group)
+    def exchange(h):
+        there = (slice(None), h // 2, pl.ds((h % 2) * tall, tall))
+        return remote(give.at[there], got.at[there], ex_s.at[h], ex_r.at[h], partner)
+
+    for h in range(parts):
+        scaled(h, col_p, first_p, give)
+        exchange(h).start()
     load_wm.wait()
-    loop(0, n, functools.partial(scaled, col_m, first, mine))
-
-    for q in range(groups):
-        exchange(q).wait_recv()
-
-    def merge(i):
-        tiles = pl.ds(2 * i, 2)
-        mine[tiles] = mine[tiles] + got[tiles]
-
-    loop(0, n - 1, merge)
-    r1[first] = mine[pl.ds(2 * n - 2, 2)] + got[pl.ds(2 * n - 2, 2)]
-    high = 2
 
     def strip(h):
-        return lax.div(h, high), pl.ds(pl.multiple_of(lax.rem(h, high) * tall, 16), tall)
-
-    def send_first(j):
-        h, i = lax.div(j, n - 1), lax.rem(j, n - 1)
-        t = lax.rem(first + nth(i, n), n)
-        k, span = strip(h)
-        remote(
-            mine.at[2 * i + k, span], r1.at[first, k, span], s1_s.at[t], s1_r.at[first, h],
-            along_first(t),
-        ).start()
-
-    loop(0, parts * (n - 1), send_first)
+        return lax.div(h, 2), pl.ds(pl.multiple_of(lax.rem(h, 2) * tall, 16), tall)
+
+    for h in range(parts):
+        scaled(h, col_m, first, mine)
+        exchange(h).wait_recv()
+        k, span = h // 2, pl.ds((h % 2) * tall, tall)
+
+        def send_first(i):
+            t = lax.rem(first + nth(i, n), n)
+            mine[i, k, span, :] = mine[i, k, span, :] + got[i, k, span, :]
+            remote(
+                mine.at[i, k, span], r1.at[first, k, span], s1_s.at[t], s1_r.at[first, h],
+                along_first(t),
+            ).start()
+
+        loop(0, n - 1, send_first)
+        r1[first, k, span, :] = mine[n - 1, k, span, :] + got[n - 1, k, span, :]
 
     load_ao.wait()
     load_oc.wait()
@@ -436,10 +430,8 @@
         piece = piece + ryh[p].astype(F32)
     y_help[...] = piece.astype(BF16)
 
-    def drain_exchange(q):
-        exchange(q).wait_send()
-
-    loop(0, groups, drain_exchange)
+    for h in range(parts):
+        exchange(h).wait_send()
 
     def drain_mate(d):
         j = lax.rem(me + d, 8)
@@ -530,8 +522,6 @@
         rows, hrows = act_own.shape[1], act_help.shape[1]
         half, zblock, wide = depth // 2, depth // nz, depth // 8
         owners, cols = n * n // 4, depth // (2 * n * n)
-        tiles = half // LANES
-        groups = min(4, n)
         vmem = pltpu.VMEM
         dma = pltpu.SemaphoreType.DMA
         smem = pl.BlockSpec(memory_space=pltpu.SMEM)
@@ -563,9 +553,9 @@
                 vmem((rows, ff), BF16),
                 vmem((8, hrows, ff), BF16),
                 vmem((8, hrows, wide), BF16),
-                vmem((tiles, ff, LANES), BF16),
-                vmem((tiles, ff, LANES), BF16),
-                vmem((tiles, ff, LANES), BF16),
+                vmem((n, 2, ff, LANES), BF16),
+                vmem((n, 2, ff, LANES), BF16),
+                vmem((n, 2, ff, LANES), BF16),
                 vmem((n, 2, ff, LANES), BF16),
                 vmem((2, ff, LANES), BF16),
                 vmem((n, 2, ff, LANES), BF16),
@@ -579,7 +569,7 @@
                 vmem((8, hrows, ff), BF16),
                 vmem((8, hrows, ff), BF16),
                 dma((10,)),
-                dma((groups,)), dma((groups,)),
+                dma((4,)), dma((4,)),
                 dma((8,)), dma((8,)),
                 dma((8,)), dma((8,)),
                 dma((nz,)), dma((nz,)),

time: 72 us -> 71.8 us (level)
  no operation moved by 1% of the time
where the time goes in v4:
time: 71.8 us; the launch traced here: 71.6 us
  Pallas kernels  69 us (96%)
  between operations  2.58 us (4%)
    pallas_call x1, Pallas kernels, body(): pl.pallas_call(functools.partial(kernel, (n, nz, ff, rows, hrows, depth))...  66.1 us
    pallas_call x1, Pallas kernels, body(): pl.pallas_call(finish, out_shape=(jax.ShapeDtypeStruct((ff, depth), BF16)...  2.99 us

profile of v4, /device:TPU:1, one launch (start us, length us, event | category | flops | bytes accessed | tf_op | source)
XLA Modules:
  0.0 71.6 jit_solution(9881761869367116172)
XLA Ops:
  2.6 66.1 %moe_step.1 = (bf16[128,512]{1,0:T(8,128)(2,1)}, bf16[192,128]{1,0:T(8,128)(2,1)}, bf16[32,512]{1,0:T(8,128)(2,1)}, bf16[32,192]{1,0:T(8,128)(2,1)}, f32[32,192]{1,0:T(8,128)}) custom-call(s32[1]{0:T(128)S(6)} %copy.17.hot_h, s32[1]{0:T(128)S(6)} %copy.15.own_count_h.refs_0_, s32[1]{0:T(128)S(6)} %copy.16.help_count_h, f32[12,1,32]{2,1,0:T(1,128)} %bitcast.23, ...), custom_call_target="tpu_custom_call" | custom-call | tf_op jit(solution)/shard_map/moe_step/pallas_call | solution.py:538
  68.6 3.0 %finish.1 = (bf16[192,4096]{1,0:T(8,128)(2,1)}, bf16[128,512]{1,0:T(8,128)(2,1)}, bf16[192,128]{1,0:T(8,128)(2,1)}, bf16[32,512]{1,0:T(8,128)(2,1)}, bf16[32,192]{1,0:T(8,128)(2,1)}, /*index=5*/f32[32,192]{1,0:T(8,128)}) custom-call(s32[1]{0:T(128)S(6)} %copy.15.own_count_h.refs_0_, bf16[192,128]{1,0:T(8,128)(2,1)} %bitcast.21, bf16[128,4096]{1,0:T(8,128)(2,1)} %bitcast.17, ...), custom_call_target="tpu_custom_call" | custom-call | tf_op jit(solution)/shard_map/finish/pallas_call | solution.py:589
